TPU v7x, 512 devices: a whole 4x8x8 slice. The times are simulated.
512 devices in a mesh: ctx: 64 (over z, y), tp: 4 (over x), dp: 2 (over core).
Axes of the slice: x: 4, y: 8, z: 8, core: 2. Of those that a mesh axis runs over, the one named last changes fastest.
Arguments:
- projected: bfloat16 [3, 2, 16384, 1024], P(None, 'dp', 'ctx', 'tp'), may hold values from -6 to 6
- segment_ids: int32 [2, 16384], P('dp', 'ctx'), may hold values from 0 to 31, never falling along the last dimension, each value on 1 to 768 neighbouring positions
- short_filter: float32 [3, 3, 1024], P(None, None, 'tp'), may hold values from -3.5 to 3.5
- long_filter: float32 [64, 16384], P('tp', 'ctx'), may hold values from -4 to 4
- out_proj: bfloat16 [1024, 1024], P('tp'), may hold values from -0.1875 to 0.1875
- mixed_cotangent: bfloat16 [2, 16384, 1024], P('dp', 'ctx', 'tp'), may hold values from -6 to 6
Outputs:
- mixed: bfloat16 [2, 16384, 1024], P('dp', 'ctx', 'tp')
- grad_projected: bfloat16 [3, 2, 16384, 1024], P(None, 'dp', 'ctx', 'tp')
- grad_short: float32 [3, 3, 1024], P(None, None, 'tp')
- grad_long: float32 [64, 16384], P('tp', 'ctx')
- grad_out_proj: float32 [1024, 1024], P('tp')
Inputs may be any that keep to these rules, and one draw needn't show every extreme that they name: `segment_ids`: along each window the id never falls; every id covers 1 to 768 consecutive positions, and one covers exactly 768.
All inputs are finite; a program needn't handle non-finite values.
Results may differ from a plain program's by a relative error of at most 0.0049.
Values may be sent and summed in bfloat16 or wider, within the bound.
A program may use at most 64 MiB of HBM per device.

v0:
```python
import math

import jax
import jax.numpy as jnp
from jax import lax
from jax.sharding import PartitionSpec as P

highest_precision = lax.Precision.HIGHEST


def shifted(value, axis, steps):
    count = lax.axis_size(axis)
    first, last = (max(0, -steps), min(count, count - steps))
    return lax.ppermute(value, axis, [(source, source + steps) for source in range(first, last)])


def angle_table(height, breadth, period, direction):
    product = (
        jnp.arange(height, dtype=jnp.int32)[:, None]
        * jnp.arange(breadth, dtype=jnp.int32)[None, :]
        % period
    )
    angles = direction * 2.0 * math.pi / period * product.astype(jnp.float32)
    return (jnp.cos(angles), jnp.sin(angles))


def row_twiddle(spec_re, spec_im, direction):
    my_index = lax.axis_index("ctx")
    devices = lax.axis_size("ctx")
    row_count = spec_re.shape[1]
    period = 2 * devices * row_count
    freq_pair = 2 * my_index + jnp.arange(2, dtype=jnp.int32)
    product = freq_pair[:, None] * jnp.arange(row_count, dtype=jnp.int32)[None, :] % period
    angles = direction * 2.0 * math.pi / period * product.astype(jnp.float32)
    cosine = jnp.cos(angles)[:, :, None]
    sine_part = jnp.sin(angles)[:, :, None]
    return (spec_re * cosine - spec_im * sine_part, spec_re * sine_part + spec_im * cosine)


def row_transform(spec_re, spec_im, direction):
    row_count = spec_re.shape[1]
    cosine, sine_part = angle_table(row_count, row_count, row_count, direction)

    def along_rows(blocks, matrix):
        return jnp.einsum("kmc,mq->kqc", blocks, matrix, precision=highest_precision)

    return (
        along_rows(spec_re, cosine) - along_rows(spec_im, sine_part),
        along_rows(spec_re, sine_part) + along_rows(spec_im, cosine),
    )


def mixing(matrix, blocks):
    return jnp.einsum("kj,jmc->kmc", matrix, blocks, precision=highest_precision)


def forward_spectrum(real_part):
    devices = lax.axis_size("ctx")
    cosine, sine_part = angle_table(2 * devices, devices, 2 * devices, -1.0)
    spread_re = lax.all_to_all(real_part[None], "ctx", split_axis=1, concat_axis=0, tiled=True)
    column_re = mixing(cosine, spread_re)
    column_im = mixing(sine_part, spread_re)
    near_re, near_im = (
        lax.all_to_all(column_re, "ctx", split_axis=0, concat_axis=1, tiled=True),
        lax.all_to_all(column_im, "ctx", split_axis=0, concat_axis=1, tiled=True),
    )
    twist_re, twist_im = row_twiddle(near_re, near_im, -1.0)
    return row_transform(twist_re, twist_im, -1.0)


def inverse_spectrum(spec_re, spec_im):
    devices = lax.axis_size("ctx")
    row_count = spec_re.shape[1]
    back_re, back_im = row_transform(spec_re, spec_im, 1.0)
    twist_re, twist_im = row_twiddle(back_re / row_count, back_im / row_count, 1.0)
    far_re, far_im = (
        lax.all_to_all(twist_re, "ctx", split_axis=1, concat_axis=0, tiled=True),
        lax.all_to_all(twist_im, "ctx", split_axis=1, concat_axis=0, tiled=True),
    )
    cosine, sine_part = angle_table(devices, 2 * devices, 2 * devices, 1.0)
    out_re = (mixing(cosine, far_re) - mixing(sine_part, far_im)) / (2 * devices)
    rows_re = lax.all_to_all(out_re, "ctx", split_axis=0, concat_axis=1, tiled=True)
    return (rows_re[0], rows_re[0])


def pack_columns(values):
    return (values, values)


def by_filter(val_re, val_im, fil_re, fil_im, conjugate):
    val_shape = val_re.shape
    group_count = fil_re.shape[2]
    v_re = val_re.reshape(val_shape[0], val_shape[1], group_count, -1)
    v_im = val_im.reshape(val_shape[0], val_shape[1], group_count, -1)
    f_re = fil_re[:, :, :, None]
    f_im = fil_im[:, :, :, None]
    if conjugate:
        f_im = -f_im
    out_re = v_re * f_re - v_im * f_im
    out_im = v_re * f_im + v_im * f_re
    return (out_re.reshape(val_shape), out_im.reshape(val_shape))


def short_local(extended, filters, seg_ext):
    reach_taps = filters.shape[1]
    out_rows = extended.shape[1] - reach_taps + 1
    own_seg = seg_ext[reach_taps - 1 :]
    running = jnp.zeros((extended.shape[0], out_rows, extended.shape[2]), jnp.float32)
    for shift_by in range(reach_taps):
        start_row = reach_taps - 1 - shift_by
        same_doc = jnp.where(seg_ext[start_row : start_row + out_rows] == own_seg, 1.0, 0.0)
        running = (
            running
            + filters[:, shift_by][:, None, :]
            * same_doc[None, :, None]
            * extended[:, start_row : start_row + out_rows]
        )
    return running


def per_device(projected, segment_ids, short_filter, long_filter, out_proj, mixed_cotangent):
    row_count = projected.shape[2]
    stacked = projected.shape[0]
    width_dev = projected.shape[3]
    short_reach = short_filter.shape[1]
    group_count = long_filter.shape[0]
    grad_scale = 1.0 / math.sqrt(
        projected.shape[1] * lax.axis_size("dp") * row_count * lax.axis_size("ctx")
    )
    segments = segment_ids[0]
    source = projected[:, 0]
    short_rows = short_reach - 1
    cot_full = lax.all_gather(mixed_cotangent[0], "tp", axis=1, tiled=True)
    prev_tail, prev_seg = shifted(
        (source[:, row_count - short_rows :], segments[row_count - short_rows :]), "ctx", 1
    )
    short_seg = jnp.concatenate([prev_seg, segments])
    short_ext = jnp.concatenate([prev_tail, source], axis=1).astype(jnp.float32)

    def short_piece(extended, filters):
        return short_local(extended, filters, short_seg)

    short_out, short_pull = jax.vjp(short_piece, short_ext, short_filter)
    query_conv = short_out[0]
    gated_rows = short_out[1] * short_out[2]
    filter_cols = long_filter.T
    mid_re, mid_im = pack_columns(gated_rows)
    spec_re, spec_im = forward_spectrum(jnp.concatenate([mid_re, filter_cols], axis=1))
    data_cols = spec_re.shape[2] - group_count
    signal_re = spec_re[:, :, :data_cols]
    signal_im = spec_im[:, :, :data_cols]
    filt_re = spec_re[:, :, data_cols:]
    filt_im = spec_im[:, :, data_cols:]
    long_re, long_im = by_filter(signal_re, signal_im, filt_re, filt_im, False)
    out_re, out_im = inverse_spectrum(long_re, long_im)
    y_out = (query_conv * out_re).astype(jnp.bfloat16)
    partial_out = jnp.dot(y_out, out_proj, preferred_element_type=jnp.float32)
    mixed = lax.psum_scatter(partial_out, "tp", scatter_dimension=1, tiled=True).astype(
        jnp.bfloat16
    )
    grad_y = jnp.dot(cot_full, out_proj.T, preferred_element_type=jnp.float32)
    grad_proj_local = jnp.dot(y_out.T, cot_full, preferred_element_type=jnp.float32)
    grad_long_out = grad_y * query_conv
    grad_query = grad_y * out_re
    grad_in_re, grad_in_im = pack_columns(grad_long_out)
    cot_re, cot_im = forward_spectrum(grad_in_re)
    back_re, back_im = by_filter(cot_re, cot_im, filt_re, filt_im, True)
    cross_re = (
        (signal_re * cot_re + signal_im * cot_im).reshape(2, row_count, group_count, -1).sum(axis=3)
    )
    cross_im = (
        (signal_re * cot_im - signal_im * cot_re).reshape(2, row_count, group_count, -1).sum(axis=3)
    )
    inv_re, inv_im = inverse_spectrum(
        jnp.concatenate([back_re, cross_re], axis=2), jnp.concatenate([back_im, cross_im], axis=2)
    )
    grad_gated = inv_re[:, :data_cols]
    grad_long_local = inv_re[:, data_cols:].T
    grad_short_out = jnp.stack([grad_query, grad_gated * short_out[2], grad_gated * short_out[1]])
    grad_short_ext, grad_short_local = short_pull(grad_short_out)
    returned_short = shifted(grad_short_ext[:, :short_rows], "ctx", -1)
    grad_source = grad_short_ext[:, short_rows:] + jnp.concatenate(
        [jnp.zeros((stacked, row_count - short_rows, width_dev), jnp.float32), returned_short],
        axis=1,
    )
    total_proj, total_short = lax.psum((grad_proj_local, grad_short_local), ("ctx", "dp"))
    total_long = lax.psum(grad_long_local, "dp")
    return (
        mixed[None],
        grad_source[:, None].astype(jnp.bfloat16),
        total_short * grad_scale,
        total_long * grad_scale,
        total_proj * grad_scale,
    )


def solution(mesh):
    in_specs = (
        P(None, "dp", "ctx", "tp"),
        P("dp", "ctx"),
        P(None, None, "tp"),
        P("tp", "ctx"),
        P("tp", None),
        P("dp", "ctx", "tp"),
    )
    out_specs = (
        P("dp", "ctx", "tp"),
        P(None, "dp", "ctx", "tp"),
        P(None, None, "tp"),
        P("tp", "ctx"),
        P("tp", None),
    )
    return jax.shard_map(
        per_device, mesh=mesh, in_specs=in_specs, out_specs=out_specs, check_vma=False
    )
```

profile of v0, /device:TPU:1, one launch (start us, length us, event | category | flops | bytes accessed | tf_op | source)
XLA Modules:
  0.0 855.0 jit_solution(18165859684335897357)
XLA Ops:
  8.8 4.0 collective-permute-start.1
  13.5 3.2 collective-permute-start
  17.6 11.7 %all-gather = bf16[1,256,1024]{2,1,0:T(8,128)(2,1)S(1)} all-gather(bf16[1,256,256]{2,1,0:T(8,128)(2,1)} %param.11), channel_id=2, replica_groups=mesh['ctx'=64,'tp'=4,'dp'=2] {'tp'}, dimensions={2}, use_global_device_ids=true | all-gather | bytes 655360 | tf_op jit(solution)/shard_map/all_gather | solution.py:133
  32.9 14.6 %all-to-all-start.6 = ((f32[1,256,256]{2,0,1:T(1,128)}), f32[1,256,256]{2,0,1:T(1,128)S(1)}, u32[]{:S(2)}, u32[]{:S(2)}) async-start(f32[1,256,256]{2,0,1:T(1,128)} %copy.152), calls=%async_computation.7 | async-start | bytes 524288 | tf_op jit(solution)/shard_map/all_to_all | solution.py:60
  48.9 11.2 %all-to-all-done.6 = f32[1,256,256]{2,0,1:T(1,128)S(1)} async-done(((f32[1,256,256]{2,0,1:T(1,128)}), f32[1,256,256]{2,0,1:T(1,128)S(1)}, u32[]{:S(2)}, u32[]{:S(2)}) %all-to-all-start.6) | async-done | bytes 262176 | tf_op jit(solution)/shard_map/all_to_all | solution.py:60
  60.0 4.6 all-to-all-start
  67.3 10.9 %all-to-all-done = f32[1,256,272]{2,0,1:T(1,128)S(1)} async-done(((f32[1,256,272]{2,0,1:T(1,128)}), f32[1,256,272]{2,0,1:T(1,128)S(1)}, u32[]{:S(2)}, u32[]{:S(2)}) %all-to-all-start) | async-done | bytes 278560 | tf_op jit(solution)/shard_map/all_to_all | solution.py:60
  78.2 4.6 all-to-all-start.7
  84.7 12.7 %all-to-all-done.7 = f32[128,4,256]{2,1,0:T(4,128)S(1)} async-done(((f32[128,4,256]{2,1,0:T(4,128)}), f32[128,4,256]{2,1,0:T(4,128)S(1)}, u32[]{:S(2)}, u32[]{:S(2)}) %all-to-all-start.7) | async-done | bytes 524320 | tf_op jit(solution)/shard_map/all_to_all | solution.py:64
  98.3 5.5 all-to-all-start.8
  107.2 10.8 %all-to-all-done.8 = f32[128,4,256]{2,1,0:T(4,128)} async-done(((f32[128,4,256]{2,1,0:T(4,128)}), f32[128,4,256]{2,1,0:T(4,128)}, u32[]{:S(2)}, u32[]{:S(2)}) %all-to-all-start.8) | async-done | bytes 524320 | tf_op jit(solution)/shard_map/all_to_all | solution.py:65
  118.0 5.0 all-to-all-start.1
  123.0 2.0 fusion.31
  125.0 2.2 copy.132
  127.2 12.9 %all-to-all-done.1 = f32[128,4,272]{2,1,0:T(4,128)S(1)} async-done(((f32[128,4,272]{2,1,0:T(4,128)}), f32[128,4,272]{2,1,0:T(4,128)S(1)}, u32[]{:S(2)}, u32[]{:S(2)}) %all-to-all-start.1) | async-done | bytes 557088 | tf_op jit(solution)/shard_map/all_to_all | solution.py:64
  140.1 6.0 all-to-all-start.2
  148.2 1.4 copy.159
  149.6 1.5 fusion.23
  153.4 2.7 fusion.42
  156.1 2.4 fusion.49
  158.4 2.4 fusion.4
  160.8 1.3 copy.129
  162.8 1.6 copy.133
  164.4 1.8 fusion.14
  167.4 3.6 fusion.52
  171.0 2.4 fusion.45
  173.4 1.5 copy.136
  174.9 2.7 fusion.3
  177.7 1.6 fusion.2
  179.3 1.8 bitcast_reduce_fusion
  182.4 1.9 fusion.57
  184.3 1.9 fusion.39
  186.2 1.9 fusion.7
  188.2 2.2 multiply_add_fusion.2
  191.6 11.4 %all-to-all-start.3 = ((f32[2,256,256]{2,0,1:T(2,128)}), f32[2,256,256]{2,0,1:T(2,128)S(1)}, u32[]{:S(2)}, u32[]{:S(2)}) async-start(f32[2,256,256]{2,0,1:T(2,128)} %copy.147), calls=%async_computation.3 | async-start | bytes 1048576 | tf_op jit(solution)/shard_map/all_to_all | solution.py:77
  204.3 13.2 %all-to-all-done.3 = f32[2,256,256]{2,0,1:T(2,128)S(1)} async-done(((f32[2,256,256]{2,0,1:T(2,128)}), f32[2,256,256]{2,0,1:T(2,128)S(1)}, u32[]{:S(2)}, u32[]{:S(2)}) %all-to-all-start.3) | async-done | bytes 524320 | tf_op jit(solution)/shard_map/all_to_all | solution.py:77
  218.2 5.5 all-to-all-start.4
  223.7 1.6 fusion.28
  225.4 1.6 fusion.29
  227.0 1.6 fusion.1
  228.6 1.7 multiply_add_fusion
  231.5 6.5 all-to-all-done.4
  238.0 5.8 all-to-all-start.9
  244.9 15.2 %all-to-all-done.9 = f32[2,256,272]{2,0,1:T(2,128)S(1)} async-done(((f32[2,256,272]{2,0,1:T(2,128)}), f32[2,256,272]{2,0,1:T(2,128)S(1)}, u32[]{:S(2)}, u32[]{:S(2)}) %all-to-all-start.9) | async-done | bytes 557088 | tf_op jit(solution)/shard_map/all_to_all | solution.py:77
  260.2 5.7 all-to-all-start.10
  266.8 1.4 all_to_all.149
  268.2 2.0 copy.209
  270.2 2.2 all_to_all.153
  276.0 6.1 all-to-all-done.10
  282.1 6.0 all-to-all-start.5
  288.1 1.4 copy.169
  291.9 8.7 %all-to-all-done.5 = f32[64,4,256]{2,1,0:T(4,128)S(1)} async-done(((f32[64,4,256]{2,1,0:T(4,128)}), f32[64,4,256]{2,1,0:T(4,128)S(1)}, u32[]{:S(2)}, u32[]{:S(2)}) %all-to-all-start.5) | async-done | bytes 262176 | tf_op jit(solution)/shard_map/all_to_all | solution.py:82
  300.6 4.6 all-to-all-start.11
  306.1 12.7 %all-to-all-done.11 = f32[64,4,272]{2,1,0:T(4,128)S(1)} async-done(((f32[64,4,272]{2,1,0:T(4,128)}), f32[64,4,272]{2,1,0:T(4,128)S(1)}, u32[]{:S(2)}, u32[]{:S(2)}) %all-to-all-start.11) | async-done | bytes 278560 | tf_op jit(solution)/shard_map/all_to_all | solution.py:82
  319.6 1.2 multiply_bitcast_fusion.1
  320.9 1.3 fusion.24
  322.3 1.3 fusion.235
  324.3 1.6 multiply_reduce_fusion.2
  325.9 1.4 collective-permute-start.2
  327.3 501.3 %psum.21 = f32[3,3,256]{2,0,1:T(4,128)S(1)} all-reduce(f32[3,3,256]{2,0,1:T(4,128)S(1)} %pad_add_fusion.1), channel_id=1, replica_groups=mesh['ctx'=64,'tp'=4,'dp'=2] {'ctx','dp'}, use_global_device_ids=true, to_apply=%region_6.7 | all-reduce | flops 2304 | bytes 18432 | tf_op jit(solution)/shard_map/psum | solution.py:186
  829.5 9.2 %psum.22 = f32[16,256]{0,1:T(8,128)S(1)} all-reduce(f32[16,256]{0,1:T(8,128)S(1)} %slice_bitcast_fusion.3), channel_id=1, replica_groups=mesh['ctx'=64,'tp'=4,'dp'=2] {'dp'}, use_global_device_ids=true, to_apply=%region_7.8 | all-reduce | flops 4096 | bytes 32768 | tf_op jit(solution)/shard_map/psum | solution.py:187
  841.2 2.0 fusion.30
  843.2 2.3 broadcast_multiply_fusion
  845.5 1.6 convert_bitcast_fusion
  (131 shorter events, 41.4 us)
Async XLA Ops:
  8.0 21.3 %copy-start = (bf16[256,1024]{1,0:T(8,128)(2,1)S(1)}, bf16[256,1024]{1,0:T(8,128)(2,1)}, u32[]{:S(2)}) copy-start(bf16[256,1024]{1,0:T(8,128)(2,1)} %param.10) | copy-start | bytes 1572868
  8.8 21.3 %collective-permute-start.1 = (s32[2]{0:T(128)S(1)}, s32[2]{0:T(128)S(1)}, u32[]{:S(2)}, u32[]{:S(2)}) collective-permute-start(s32[2]{0:T(128)S(1)} %slice_bitcast_fusion.4), channel_id=1, source_target_pairs={{0,8},{8,16},{16,24},{24,32},{32,40},{40,48},{48,56},{56,64},{64,7... | collective-permute-start | bytes 32 | tf_op jit(solution)/shard_map/ppermute | solution.py:14
  13.5 17.4 %collective-permute-start = (bf16[3,2,256]{2,1,0:T(2,128)(2,1)S(1)}, bf16[3,2,256]{2,1,0:T(2,128)(2,1)S(1)}, u32[]{:S(2)}, u32[]{:S(2)}) collective-permute-start(bf16[3,2,256]{2,1,0:T(2,128)(2,1)S(1)} %slice.90), channel_id=1, source_target_pairs={{0,8},{8,16},{16,24},{24,32},{32,40},{40,48},{48,56},{56,64},{64,7... | collective-permute-start | bytes 9224 | tf_op jit(solution)/shard_map/ppermute | solution.py:14
  29.3 0.8 copy-start.3
  29.3 1.6 copy-start.26
  30.1 1.7 copy-start.8
  30.1 0.7 copy-start.30
  30.9 0.6 copy-start.28
  32.9 14.7 %copy-start.27 = (f32[16,256]{1,0:T(8,128)S(1)}, f32[16,256]{1,0:T(8,128)}, u32[]{:S(2)}) copy-start(f32[16,256]{1,0:T(8,128)} %param.9) | copy-start | bytes 49156
  32.9 27.1 %all-to-all-start.6 = ((f32[1,256,256]{2,0,1:T(1,128)}), f32[1,256,256]{2,0,1:T(1,128)S(1)}, u32[]{:S(2)}, u32[]{:S(2)}) async-start(f32[1,256,256]{2,0,1:T(1,128)} %copy.152), calls=%async_computation.7 | async-start | bytes 524288 | tf_op jit(solution)/shard_map/all_to_all | solution.py:60
  60.0 18.1 %all-to-all-start = ((f32[1,256,272]{2,0,1:T(1,128)}), f32[1,256,272]{2,0,1:T(1,128)S(1)}, u32[]{:S(2)}, u32[]{:S(2)}) async-start(f32[1,256,272]{2,0,1:T(1,128)} %copy.126), calls=%async_computation | async-start | bytes 786432 | tf_op jit(solution)/shard_map/all_to_all | solution.py:60
  78.2 19.3 %all-to-all-start.7 = ((f32[128,4,256]{2,1,0:T(4,128)}), f32[128,4,256]{2,1,0:T(4,128)S(1)}, u32[]{:S(2)}, u32[]{:S(2)}) async-start(f32[128,4,256]{2,1,0:T(4,128)} %copy.154), calls=%async_computation.8 | async-start | bytes 1048576 | tf_op jit(solution)/shard_map/all_to_all | solution.py:64
  97.4 0.8 copy-start.11
  98.3 19.7 %all-to-all-start.8 = ((f32[128,4,256]{2,1,0:T(4,128)}), f32[128,4,256]{2,1,0:T(4,128)}, u32[]{:S(2)}, u32[]{:S(2)}) async-start(f32[128,4,256]{2,1,0:T(4,128)} %copy.158), calls=%async_computation.9 | async-start | bytes 1048576 | tf_op jit(solution)/shard_map/all_to_all | solution.py:65
  118.0 22.1 %all-to-all-start.1 = ((f32[128,4,272]{2,1,0:T(4,128)}), f32[128,4,272]{2,1,0:T(4,128)S(1)}, u32[]{:S(2)}, u32[]{:S(2)}) async-start(f32[128,4,272]{2,1,0:T(4,128)} %copy.128), calls=%async_computation.1 | async-start | bytes 1572864 | tf_op jit(solution)/shard_map/all_to_all | solution.py:64
  140.1 7.8 copy-start.12
  140.1 22.7 %all-to-all-start.2 = ((f32[128,4,272]{2,1,0:T(4,128)}), f32[128,4,272]{2,1,0:T(4,128)}, u32[]{:S(2)}, u32[]{:S(2)}) async-start(f32[128,4,272]{2,1,0:T(4,128)} %copy.132), calls=%async_computation.2 | async-start | bytes 1572864 | tf_op jit(solution)/shard_map/all_to_all | solution.py:65
  148.2 1.4 copy-start.17
  148.2 1.4 copy-start.19
  153.3 2.7 copy-start.24
  162.8 1.6 copy-start.7
  162.8 1.6 copy-start.18
  162.8 1.7 copy-start.20
  167.4 3.6 copy-start.22
  174.9 2.7 copy-start.21
  177.7 1.7 copy-start.5
  177.7 1.7 copy-start.23
  191.6 25.8 %all-to-all-start.3 = ((f32[2,256,256]{2,0,1:T(2,128)}), f32[2,256,256]{2,0,1:T(2,128)S(1)}, u32[]{:S(2)}, u32[]{:S(2)}) async-start(f32[2,256,256]{2,0,1:T(2,128)} %copy.147), calls=%async_computation.3 | async-start | bytes 1048576 | tf_op jit(solution)/shard_map/all_to_all | solution.py:77
  204.3 19.5 %copy-start.25 = (f32[2,256,256]{1,2,0:T(8,128)S(1)}, f32[2,256,256]{1,2,0:T(8,128)}, u32[]{:S(2)}) copy-start(f32[2,256,256]{1,2,0:T(8,128)} %get-tuple-element.41) | copy-start | bytes 1572868
  217.4 0.8 copy-start.13
  218.2 19.7 %all-to-all-start.4 = ((f32[2,256,256]{2,0,1:T(2,128)}), f32[2,256,256]{2,0,1:T(2,128)}, u32[]{:S(2)}, u32[]{:S(2)}) async-start(f32[2,256,256]{2,0,1:T(2,128)} %copy.149), calls=%async_computation.4 | async-start | bytes 1048576 | tf_op jit(solution)/shard_map/all_to_all | solution.py:78
  225.4 1.6 copy-start.16
  238.0 22.2 %all-to-all-start.9 = ((f32[2,256,272]{2,0,1:T(2,128)}), f32[2,256,272]{2,0,1:T(2,128)S(1)}, u32[]{:S(2)}, u32[]{:S(2)}) async-start(f32[2,256,272]{2,0,1:T(2,128)} %copy.165), calls=%async_computation.10 | async-start | bytes 1572864 | tf_op jit(solution)/shard_map/all_to_all | solution.py:77
  244.9 20.9 %copy-start.14 = (f32[2,256,256]{2,0,1:T(2,128)S(1)}, f32[2,256,256]{2,0,1:T(2,128)}, u32[]{:S(2)}) copy-start(f32[2,256,256]{2,0,1:T(2,128)} %copy-done.13) | copy-start | bytes 1572868
  260.2 22.0 %all-to-all-start.10 = ((f32[2,256,272]{2,0,1:T(2,128)}), f32[2,256,272]{2,0,1:T(2,128)}, u32[]{:S(2)}, u32[]{:S(2)}) async-start(f32[2,256,272]{2,0,1:T(2,128)} %copy.168), calls=%async_computation.11 | async-start | bytes 1572864 | tf_op jit(solution)/shard_map/all_to_all | solution.py:78
  272.4 1.0 copy-start.15
  282.1 18.5 %all-to-all-start.5 = ((f32[64,4,256]{2,1,0:T(4,128)}), f32[64,4,256]{2,1,0:T(4,128)S(1)}, u32[]{:S(2)}, u32[]{:S(2)}) async-start(f32[64,4,256]{2,1,0:T(4,128)} %copy.151), calls=%async_computation.5 | async-start | bytes 524288 | tf_op jit(solution)/shard_map/all_to_all | solution.py:82
  288.1 1.4 copy-start.6
  300.6 18.2 %all-to-all-start.11 = ((f32[64,4,272]{2,1,0:T(4,128)}), f32[64,4,272]{2,1,0:T(4,128)S(1)}, u32[]{:S(2)}, u32[]{:S(2)}) async-start(f32[64,4,272]{2,1,0:T(4,128)} %copy.171), calls=%async_computation.12 | async-start | bytes 786432 | tf_op jit(solution)/shard_map/all_to_all | solution.py:82
  305.2 538.0 %all-reduce.9.cloned.1.call-start = ((), (), s32[]{:S(2)}) async-start(), calls=%async_computation.14 | async-start | bytes 2097152 | tf_op jit(solution)/shard_map/psum | solution.py:186
  306.1 13.6 %copy-start.9 = (f32[256,256]{1,0:T(8,128)S(1)}, f32[256,256]{1,0:T(8,128)}, u32[]{:S(2)}) copy-start(f32[256,256]{1,0:T(8,128)} %copy-done.8) | copy-start | bytes 786436
  319.6 1.3 copy-start.4
  320.9 2.7 copy-start.10
  322.2 523.3 %reduce-scatter.2.cloned.1.call-start = ((), (), s32[]{:S(2)}) async-start(), calls=%async_computation.13 | async-start | bytes 1310720 | tf_op jit(solution)/shard_map/reduce_scatter | solution.py:158
  323.6 0.7 copy-start.29
  324.3 1.6 copy-start.1
  325.9 512.9 %copy-start.2 = (f32[3,256,256]{2,1,0:T(8,128)S(1)}, f32[3,256,256]{2,1,0:T(8,128)}, u32[]{:S(2)}) copy-start(f32[3,256,256]{2,1,0:T(8,128)} %copy-done.1) | copy-start | bytes 2359300
  325.9 515.3 %collective-permute-start.2 = (f32[3,2,256]{2,1,0:T(2,128)S(1)}, f32[3,2,256]{2,1,0:T(2,128)S(1)}, u32[]{:S(2)}, u32[]{:S(2)}) collective-permute-start(f32[3,2,256]{2,1,0:T(2,128)S(1)} %pad_add_fusion.2), channel_id=1, source_target_pairs={{8,0},{16,8},{24,16},{32,24},{40,32},{48,40},{56,48},{64,56},{72,6... | collective-permute-start | bytes 18440 | tf_op jit(solution)/shard_map/ppermute | solution.py:14
Sparse Core Ops, SparseCore 0:
  322.3 208.3 all-reduce.8
Sparse Core Ops, SparseCore 1:
  325.5 39.9 reduce-scatter.1
where the time goes:
time: 870 us; the launch traced here: 855 us
  blocking collectives  522 us (60%)
  waiting for transfers between devices  122 us (14%)
  starting transfers between devices  88.1 us (10%)
  local copies, waits for them, and re-layouts  45.5 us (5%)
  matrix products  44.2 us (5%)
  other arithmetic  16.9 us (2%)
  between operations  16.7 us (2%)
    psum x1, blocking collectives, per_device(): lax.psum((grad_proj_local, grad_short_local), ('ctx', 'dp'))  501 us
    dot_general x16, matrix products, along_rows(): jnp.einsum('kmc,mq->kqc', blocks, matrix, precision=highest_precision)  34.1 us
    all_to_all x2, waiting for transfers between devices, inverse_spectrum(): lax.all_to_all(twist_re, 'ctx', split_axis=1, concat_axis=0, tiled=True)  28.4 us
    all_to_all x2, waiting for transfers between devices, forward_spectrum(): lax.all_to_all(column_re, 'ctx', split_axis=0, concat_axis=1, tiled=True)  25.6 us
    all_to_all x2, waiting for transfers between devices, forward_spectrum(): lax.all_to_all(real_part[None], 'ctx', split_axis=1, concat_axis=0, tiled...  22.1 us
    all_to_all x2, waiting for transfers between devices, inverse_spectrum(): lax.all_to_all(out_re, 'ctx', split_axis=0, concat_axis=1, tiled=True)  21.4 us
    all_to_all x2, starting transfers between devices, forward_spectrum(): lax.all_to_all(real_part[None], 'ctx', split_axis=1, concat_axis=0, tiled...  19.3 us
  transfers between devices with their start and end apart: 17, of which 12 were waited for; matrix products, arithmetic and copies ran while one was open for 7% of the time, Pallas kernels for 0%

commit v1 on v0

v1 whole, which is shorter than its diff:
```python
import functools
import math

import jax
import jax.numpy as jnp
from jax import lax
from jax.experimental import pallas as pl
from jax.experimental.pallas import tpu as pltpu
from jax.sharding import PartitionSpec as P

F32 = jnp.float32
BF = jnp.bfloat16
MESH = pl.DeviceIdType.MESH


def shifted(value, axis, steps):
    count = lax.axis_size(axis)
    first, last = (max(0, -steps), min(count, count - steps))
    return lax.ppermute(value, axis, [(source, source + steps) for source in range(first, last)])


def short_local(extended, filters, seg_ext):
    reach_taps = filters.shape[1]
    out_rows = extended.shape[1] - reach_taps + 1
    own_seg = seg_ext[reach_taps - 1 :]
    running = jnp.zeros((extended.shape[0], out_rows, extended.shape[2]), jnp.float32)
    for shift_by in range(reach_taps):
        start_row = reach_taps - 1 - shift_by
        same_doc = jnp.where(seg_ext[start_row : start_row + out_rows] == own_seg, 1.0, 0.0)
        running = (
            running
            + filters[:, shift_by][:, None, :]
            * same_doc[None, :, None]
            * extended[:, start_row : start_row + out_rows]
        )
    return running


def conv_kernel(x_ref, h_ref, out_ref, gl_ref, tt, lb, acc, gt, xb0, xb1, dd, hi):
    row = lax.broadcasted_iota(jnp.int32, (128, 128), 0)
    col = lax.broadcasted_iota(jnp.int32, (128, 128), 1)
    upper = col >= row

    def spread(e):
        return pltpu.roll(jnp.broadcast_to(h_ref[pl.ds(e, 1), :], (128, 128)), 0, 1, stride=1, stride_axis=0)

    def build(d, prev):
        s0 = spread(2 * d)
        a0 = jnp.where(upper, s0, prev).astype(BF)
        s1 = spread(2 * d + 1)
        a1 = jnp.where(upper, s1, s0).astype(BF)
        base = pl.multiple_of(d * 256, 256)
        tt[pl.ds(base, 128), 0:128] = a0
        tt[pl.ds(base + 128, 128), 128:256] = a0
        tt[pl.ds(base, 128), 128:256] = a1
        tt[pl.ds(base + 384, 128), 0:128] = a1
        return s1

    tt[128:256, 0:128] = jnp.zeros((128, 128), BF)
    lax.fori_loop(0, 64, build, jnp.zeros((128, 128), F32))

    x = x_ref[...].astype(F32).reshape(512, 256)
    first = lax.broadcasted_iota(jnp.int32, (8, 256), 0) < 4
    zero8 = jnp.zeros((8, 256), F32)
    mixed = jnp.concatenate(
        [jnp.where(first, x[8 * k : 8 * k + 8], x[504 - 8 * k : 512 - 8 * k]) for k in range(64)], axis=0
    )
    for e in range(4):
        if e:
            lb[:, 256 * e : 256 * e + 256] = jnp.concatenate(
                [jnp.zeros((8 * e, 256), F32), mixed[: 512 - 8 * e]], axis=0
            ).astype(BF)
        else:
            lb[:, 0:256] = mixed.astype(BF)
    for step in range(16):
        part = jnp.dot(lb[0 : 512 - 32 * step, :], tt[1024 * step : 1024 * step + 1024, :], preferred_element_type=F32)
        if step:
            acc[32 * step : 512, :] += part
        else:
            acc[...] = part
    for k in range(64):
        out_ref[k] = jnp.where(first, acc[8 * k : 8 * k + 8, :], acc[504 - 8 * k : 512 - 8 * k, :]).astype(BF)

    firsts = lax.rem(lax.broadcasted_iota(jnp.int32, (512, 256), 0), 8) < 4
    gt[...] = jnp.transpose(jnp.where(firsts, x, 0.0)).astype(BF)
    swapped = x
    moved = jnp.concatenate([x[4:], jnp.zeros((4, 256), F32)], axis=0)
    xb0[0:512, :] = moved.astype(BF)
    xb0[512:640, :] = jnp.zeros((128, 256), BF)
    xb1[0:512, :] = jnp.concatenate([moved[8:], zero8], axis=0).astype(BF)
    xb1[512:640, :] = jnp.zeros((128, 256), BF)
    dd[...] = jnp.zeros(dd.shape, F32)

    def corr(d, width, src, off):
        c = jnp.dot(gt[:, 0:width], src[pl.ds(pl.multiple_of(off, 16), width), :], preferred_element_type=F32)
        base = pl.multiple_of(d * 256, 256)
        dd[pl.ds(base, 128), :] += c[128:256, 128:256]
        dd[pl.ds(base + 128, 128), :] = c[0:128, 128:256] + c[128:256, 0:128]
        dd[pl.ds(base + 256, 128), :] = c[0:128, 0:128]

    for seg in range(4):
        width = 512 - 128 * seg

        def pair(i, carry, seg=seg, width=width):
            d = 16 * seg + 2 * i
            corr(d, width, xb0, 8 * d)
            corr(d + 1, width, xb1, 8 * d)
            return carry

        lax.fori_loop(0, 8, pair, 0)

    def fold(e, carry):
        rolled = pltpu.roll(dd[pl.ds(pl.multiple_of(e * 128 + 128, 128), 128), :], 0, 1, stride=1, stride_axis=0)
        low = jnp.where(upper, rolled, 0.0)
        gl_ref[pl.ds(e, 1), :] = jnp.sum(low, axis=0, keepdims=True)
        hi[pl.ds(e, 1), :] = jnp.sum(rolled - low, axis=0, keepdims=True)
        return carry

    hi[128:136, :] = jnp.zeros((8, 128), F32)
    lax.fori_loop(0, 128, fold, 0)
    gl_ref[...] += hi[1:129, :]


def conv(x, h):
    return pl.pallas_call(
        conv_kernel,
        out_shape=(jax.ShapeDtypeStruct((64, 8, 256), BF), jax.ShapeDtypeStruct((128, 128), F32)),
        in_specs=[pl.BlockSpec(memory_space=pltpu.VMEM)] * 2,
        out_specs=[pl.BlockSpec(memory_space=pltpu.VMEM)] * 2,
        scratch_shapes=[
            pltpu.VMEM((64 * 256 + 256, 256), BF),
            pltpu.VMEM((512, 1024), BF),
            pltpu.VMEM((512, 256), F32),
            pltpu.VMEM((256, 512), BF),
            pltpu.VMEM((640, 256), BF),
            pltpu.VMEM((640, 256), BF),
            pltpu.VMEM((130 * 128, 128), F32),
            pltpu.VMEM((136, 128), F32),
        ],
        compiler_params=pltpu.CompilerParams(vmem_limit_bytes=40 << 20),
        name="conv",
    )(x, h)


def reduce_kernel(scale, part_ref, small_ref, out_ref, osmall_ref,
                  pair_out, pair_in, s1, b1_in, s2, b2_in, g2, g1, gp,
                  sp_in, sm0, sm1, sm2, snd, rcv):
    ctx = lax.axis_index("ctx")
    dp = lax.axis_index("dp")
    y = lax.rem(ctx, 8)
    z = ctx // 8
    my1 = y * (1 - dp) + z * dp
    my2 = z * (1 - dp) + y * dp
    step1 = 1 + 7 * dp
    step2 = 8 - 7 * dp
    base1 = ctx - my1 * step1
    base2 = ctx - my2 * step2
    other = 1 - dp

    def peer1(k):
        return lax.rem(my1 + k, 8)

    def dev1(k):
        return {"ctx": base1 + peer1(k) * step1}

    def peer2(k):
        return lax.rem(my2 + k, 8)

    def dev2(k):
        return {"ctx": base2 + peer2(k) * step2}

    barrier = pltpu.get_barrier_semaphore()
    pl.semaphore_signal(barrier, 1, device_id={"dp": other}, device_id_type=MESH)
    for k in range(1, 8):
        pl.semaphore_signal(barrier, 1, device_id=dev1(k), device_id_type=MESH)
        pl.semaphore_signal(barrier, 1, device_id=dev2(k), device_id_type=MESH)
    pl.semaphore_wait(barrier, 15)

    def copy(src, dst, n, dev):
        return pltpu.make_async_remote_copy(src, dst, snd.at[n], rcv.at[n], device_id=dev, device_id_type=MESH)

    off = pl.multiple_of(other * 128, 128)
    mine = pl.multiple_of(dp * 128, 128)
    pair_out[...] = part_ref[pl.ds(off, 128), :].astype(BF)
    sm0[0] = small_ref[...]
    c0 = copy(pair_out, pair_in, 0, {"dp": other})
    c0.start()
    c1 = copy(sm0.at[0], sm0.at[1], 1, {"dp": other})
    c1.start()
    c1.wait()
    c0.wait()
    s1[...] = (part_ref[pl.ds(mine, 128), :] + pair_in[...].astype(F32)).astype(BF)
    sm1[0] = sm0[0] + sm0[1]

    def rows(k):
        return pl.ds(pl.multiple_of(k * 16, 16), 16)

    def cols(k):
        return pl.ds(pl.multiple_of(k * 128, 128), 128)

    cs = []
    for k in range(1, 8):
        c = copy(s1.at[rows(peer1(k)), :], b1_in.at[k], 1 + k, dev1(k)); c.start(); cs.append(c)
        c = copy(sm1.at[0], sm1.at[k], 8 + k, dev1(k)); c.start(); cs.append(c)
    for c in cs:
        c.wait()
    tot = s1[rows(my1), :].astype(F32)
    small = sm1[0]
    for k in range(1, 8):
        tot += b1_in[k].astype(F32)
    for k in range(1, 8):
        small += sm1[k]
    s2[...] = tot.astype(BF)
    sm2[0] = small
    cs = []
    for k in range(1, 8):
        c = copy(s2.at[:, cols(peer2(k))], b2_in.at[k], 15 + k, dev2(k)); c.start(); cs.append(c)
        c = copy(sm2.at[0], sm2.at[k], 22 + k, dev2(k)); c.start(); cs.append(c)
    for c in cs:
        c.wait()
    tot = s2[:, cols(my2)].astype(F32)
    small = sm2[0]
    for k in range(1, 8):
        tot += b2_in[k].astype(F32)
    for k in range(1, 8):
        small += sm2[k]
    osmall_ref[...] = small * scale
    g2[:, cols(my2)] = (tot * scale).astype(BF)
    cs = []
    for k in range(1, 8):
        c = copy(g2.at[:, cols(my2)], g2.at[:, cols(my2)], 29 + k, dev2(k)); c.start(); cs.append(c)
    for c in cs:
        c.wait()
    g1[rows(my1), :] = g2[...]
    cs = []
    for k in range(1, 8):
        c = copy(g1.at[rows(my1), :], g1.at[rows(my1), :], 36 + k, dev1(k)); c.start(); cs.append(c)
    for c in cs:
        c.wait()
    c0 = copy(g1, gp, 44, {"dp": other})
    c0.start()
    out_ref[pl.ds(mine, 128), :] = g1[...].astype(F32)
    c0.wait()
    out_ref[pl.ds(off, 128), :] = gp[...].astype(F32)


def reduce_all(part, small, scale):
    return pl.pallas_call(
        functools.partial(reduce_kernel, scale),
        out_shape=(jax.ShapeDtypeStruct((256, 1024), F32), jax.ShapeDtypeStruct((16, 256), F32)),
        in_specs=[pl.BlockSpec(memory_space=pltpu.VMEM)] * 2,
        out_specs=[pl.BlockSpec(memory_space=pltpu.VMEM)] * 2,
        scratch_shapes=[
            pltpu.VMEM((128, 1024), BF), pltpu.VMEM((128, 1024), BF), pltpu.VMEM((128, 1024), BF),
            pltpu.VMEM((8, 16, 1024), BF), pltpu.VMEM((16, 1024), BF), pltpu.VMEM((8, 16, 128), BF),
            pltpu.VMEM((16, 1024), BF), pltpu.VMEM((128, 1024), BF), pltpu.VMEM((128, 1024), BF),
            pltpu.VMEM((8, 128), F32), pltpu.VMEM((2, 16, 256), F32), pltpu.VMEM((8, 16, 256), F32), pltpu.VMEM((8, 16, 256), F32),
            pltpu.SemaphoreType.DMA((45,)), pltpu.SemaphoreType.DMA((45,)),
        ],
        compiler_params=pltpu.CompilerParams(vmem_limit_bytes=24 << 20, collective_id=0, has_side_effects=True),
        name="reduce_all",
    )(part, small)


def lanes_first(block):
    return block.T.reshape(64, 4, 256)


def per_device(projected, segment_ids, short_filter, long_filter, out_proj, mixed_cotangent):
    grad_scale = 1.0 / math.sqrt(2 * 256 * lax.axis_size("ctx"))
    segments = segment_ids[0]
    source = projected[:, 0]
    cot_full = lax.all_gather(mixed_cotangent[0], "tp", axis=1, tiled=True)
    filter_rows = lax.all_to_all(jnp.repeat(long_filter.astype(BF), 4, axis=0), "ctx", 0, 0, tiled=True)
    prev_tail, prev_seg = shifted((source[:, 254:], segments[254:]), "ctx", 1)
    short_seg = jnp.concatenate([prev_seg, segments])
    short_ext = jnp.concatenate([prev_tail, source], axis=1).astype(F32)
    short_out, short_pull = jax.vjp(lambda e, f: short_local(e, f, short_seg), short_ext, short_filter)
    query_conv = short_out[0]
    gated_rows = (short_out[1] * short_out[2]).astype(BF)
    grad_y = lax.dot_general(cot_full, out_proj, (((1,), (1,)), ((), ())), preferred_element_type=F32)
    grad_long_out = (grad_y * query_conv).astype(BF)
    sent = jnp.concatenate([lanes_first(gated_rows), lanes_first(grad_long_out[::-1])], axis=1)
    got = lax.all_to_all(sent, "ctx", 0, 0, tiled=True)
    conv_out, long_part = conv(got, filter_rows.astype(F32).reshape(128, 128))
    back = lax.all_to_all(conv_out, "ctx", 0, 0, tiled=True)
    long_back = lax.all_to_all(long_part.reshape(64, 256).astype(BF), "ctx", 0, 0, tiled=True)
    long_out = back[:, :4].reshape(256, 256).T.astype(F32)
    grad_gated = back[:, 4:].reshape(256, 256).T[::-1].astype(F32)
    grad_long_local = long_back.astype(F32).reshape(16, 4, 2, 128).sum(axis=1)[:, :, ::-1].reshape(16, 256)
    y_out = (query_conv * long_out).astype(BF)
    partial_out = jnp.dot(y_out, out_proj, preferred_element_type=F32)
    mixed = lax.psum_scatter(partial_out, "tp", scatter_dimension=1, tiled=True).astype(BF)
    grad_proj_local = jnp.dot(y_out.T, cot_full, preferred_element_type=F32)
    grad_query = grad_y * long_out
    grad_short_out = jnp.stack([grad_query, grad_gated * short_out[2], grad_gated * short_out[1]])
    grad_short_ext, grad_short_local = short_pull(grad_short_out)
    returned_short = shifted(grad_short_ext[:, :2], "ctx", -1)
    grad_source = grad_short_ext[:, 2:] + jnp.concatenate([jnp.zeros((3, 254, 256), F32), returned_short], axis=1)
    small = jnp.concatenate([grad_short_local.reshape(9, 256), jnp.zeros((7, 256), F32)], axis=0)
    total_proj, total_small = reduce_all(grad_proj_local, small, grad_scale)
    total_long = lax.psum(grad_long_local, "dp")
    return (
        mixed[None],
        grad_source[:, None].astype(BF),
        total_small[:9].reshape(3, 3, 256),
        total_long * grad_scale,
        total_proj,
    )


def solution(mesh):
    in_specs = (
        P(None, "dp", "ctx", "tp"),
        P("dp", "ctx"),
        P(None, None, "tp"),
        P("tp", "ctx"),
        P("tp", None),
        P("dp", "ctx", "tp"),
    )
    out_specs = (
        P("dp", "ctx", "tp"),
        P(None, "dp", "ctx", "tp"),
        P(None, None, "tp"),
        P("tp", "ctx"),
        P("tp", None),
    )
    return jax.shard_map(
        per_device, mesh=mesh, in_specs=in_specs, out_specs=out_specs, check_vma=False
    )
```

time: 870 us -> 203 us (0.23); the launches traced: 855 us -> 202 us
  blocking collectives: 522 us -> 54.1 us
  waiting for transfers between devices: 122 us -> 12.4 us
  Pallas kernels: 0 us -> 63 us
  starting transfers between devices: 88.1 us -> 34.6 us
  matrix products: 44.2 us -> 1.93 us
  local copies, waits for them, and re-layouts: 45.5 us -> 11.2 us
    psum x1 -> x0, blocking collectives: 501 us -> none  [per_device(): lax.psum((grad_proj_local, grad_short_local), ('ctx', 'dp'))]
    all_to_all x12 -> x2, waiting for transfers between devices: 121 us -> 12.4 us  [the longest x1 12.4 us: per_device(): got = lax.all_to_all(sent, 'ctx', 0, 0, tiled=True)]
    pallas_call x0 -> x2, Pallas kernels: none -> 63 us  [the longest x1 32.5 us: reduce_all(): pl.pallas_call(functools.partial(reduce_kernel, scale), out_shape=(jax.Sh...]
    all_to_all x12 -> x2, starting transfers between devices: 79.4 us -> 26 us  [the longest x1 14.6 us: per_device(): lax.all_to_all(jnp.repeat(long_filter.astype(BF), 4, axis=0), 'ctx', 0, 0...]
    dot_general x27 -> x3, matrix products: 44.2 us -> 1.93 us  [the longest x1 1.28 us: per_device(): partial_out = jnp.dot(y_out, out_proj, preferred_element_type=F32)]
    all_to_all x0 -> x2, blocking collectives: none -> 31 us  [the longest x1 16.3 us: per_device(): back = lax.all_to_all(conv_out, 'ctx', 0, 0, tiled=True)]
    all_to_all x12 -> x2, local copies, waits for them, and re-layouts: 13.8 us -> 0.53 us  [per_device(): lax.all_to_all(jnp.repeat(long_filter.astype(BF), 4, axis=0), 'ctx', 0, 0...]
  transfers between devices with their start and end apart: 17 -> 6, of which waited for: 12 -> 1; matrix products, arithmetic and copies ran while one was open for 7% -> 5% of each run, Pallas kernels for 0% -> 16%
where the time goes in v1:
time: 203 us; the launch traced here: 202 us
  Pallas kernels  63 us (31%)
  blocking collectives  54.1 us (27%)
  starting transfers between devices  34.6 us (17%)
  between operations  14.4 us (7%)
  waiting for transfers between devices  12.4 us (6%)
  local copies, waits for them, and re-layouts  11.2 us (6%)
  other arithmetic  10.7 us (5%)
    pallas_call x1, Pallas kernels, reduce_all(): pl.pallas_call(functools.partial(reduce_kernel, scale), out_shape=(jax.Sh...  32.5 us
    pallas_call x1, Pallas kernels, conv(): pl.pallas_call(conv_kernel, out_shape=(jax.ShapeDtypeStruct((64, 8, 256),...  30.5 us
    all_to_all x1, blocking collectives, per_device(): back = lax.all_to_all(conv_out, 'ctx', 0, 0, tiled=True)  16.3 us
    all_to_all x1, blocking collectives, per_device(): lax.all_to_all(long_part.reshape(64, 256).astype(BF), 'ctx', 0, 0, tiled=...  14.8 us
    all_to_all x1, starting transfers between devices, per_device(): lax.all_to_all(jnp.repeat(long_filter.astype(BF), 4, axis=0), 'ctx', 0, 0...  14.6 us
    all_to_all x1, waiting for transfers between devices, per_device(): got = lax.all_to_all(sent, 'ctx', 0, 0, tiled=True)  12.4 us
    psum x1, blocking collectives, per_device(): total_long = lax.psum(grad_long_local, 'dp')  11.6 us
    all_gather x1, blocking collectives, per_device(): cot_full = lax.all_gather(mixed_cotangent[0], 'tp', axis=1, tiled=True)  11.5 us
  transfers between devices with their start and end apart: 6, of which 1 were waited for; matrix products, arithmetic and copies ran while one was open for 5% of the time, Pallas kernels for 16%

profile of v1, /device:TPU:1, one launch (start us, length us, event | category | flops | bytes accessed | tf_op | source)
XLA Modules:
  0.0 202.3 jit_solution(6640746536484794099)
XLA Ops:
  7.2 0.0 copy-start
  7.2 0.8 slice_bitcast_fusion.3
  8.0 4.0 %collective-permute-start.1 = (s32[2]{0:T(128)S(1)}, s32[2]{0:T(128)S(1)}, u32[]{:S(2)}, u32[]{:S(2)}) collective-permute-start(s32[2]{0:T(128)S(1)} %slice_bitcast_fusion.3), channel_id=1, source_target_pairs={{0,8},{8,16},{16,24},{24,32},{32,40},{40,48},{48,56},{56,64},{64,7... | collective-permute-start | bytes 32 | tf_op jit(solution)/shard_map/ppermute | solution.py:19
  12.0 0.7 slice.78
  12.7 3.2 %collective-permute-start = (bf16[3,2,256]{2,1,0:T(2,128)(2,1)S(1)}, bf16[3,2,256]{2,1,0:T(2,128)(2,1)S(1)}, u32[]{:S(2)}, u32[]{:S(2)}) collective-permute-start(bf16[3,2,256]{2,1,0:T(2,128)(2,1)S(1)} %slice.78), channel_id=1, source_target_pairs={{0,8},{8,16},{16,24},{24,32},{32,40},{40,48},{48,56},{56,64},{64,7... | collective-permute-start | bytes 9224 | tf_op jit(solution)/shard_map/ppermute | solution.py:19
  15.9 0.7 convert_element_type.70
  16.7 0.0 copy-start.5
  16.7 0.5 broadcast.28
  17.2 0.8 reduce
  18.0 0.6 reshape.89
  18.7 14.6 %all-to-all-start.1 = ((bf16[64,2,128]{2,1,0:T(2,128)(2,1)}), bf16[64,2,128]{2,1,0:T(2,128)(2,1)S(1)}, u32[]{:S(2)}, u32[]{:S(2)}) async-start(bf16[64,2,128]{2,1,0:T(2,128)(2,1)} %reshape.89), calls=%async_computation.1 | async-start | bytes 65536 | tf_op jit(solution)/shard_map/all_to_all | solution.py:274
  33.3 0.0 copy-done.6
  33.4 0.0 copy-done.5
  33.4 11.5 %all-gather = bf16[1,256,1024]{2,1,0:T(8,128)(2,1)S(1)} all-gather(bf16[1,256,256]{2,1,0:T(8,128)(2,1)S(1)} %copy-done.5), channel_id=2, replica_groups=mesh['ctx'=64,'tp'=4,'dp'=2] {'tp'}, dimensions={2}, use_global_device_ids=true | all-gather | bytes 655360 | tf_op jit(solution)/shard_map/all_gather | solution.py:273
  44.9 0.0 copy-done
  44.9 0.3 fusion.5
  45.2 0.0 copy-start.7
  45.2 0.0 collective-permute-done.1
  45.2 0.7 copy-done.7
  45.9 0.1 pad_add_fusion.3
  46.0 0.1 compare_select_fusion.1
  46.1 0.0 collective-permute-done
  46.1 0.0 copy-done.4
  46.1 0.1 maximum_convert_fusion
  46.2 0.3 fusion.1
  46.5 0.1 fusion.12
  46.6 0.1 copy.27
  46.7 0.2 rev.9
  46.9 0.1 copy.28
  47.0 0.8 pad_maximum_fusion.1
  47.9 0.0 all-to-all-done.1
  47.9 11.4 %all-to-all-start = ((bf16[64,8,256]{2,1,0:T(8,128)(2,1)}), bf16[64,8,256]{2,1,0:T(8,128)(2,1)S(1)}, u32[]{:S(2)}, u32[]{:S(2)}) async-start(bf16[64,8,256]{2,1,0:T(8,128)(2,1)} %pad_maximum_fusion.1), calls=%async_computation | async-start | bytes 524288 | tf_op jit(solution)/shard_map/all_to_all | solution.py:284
  59.3 0.0 reduce-scatter.2.cloned.1.call-start
  59.3 0.1 convert_element_type.85
  59.4 12.4 %all-to-all-done.x_ref = bf16[64,8,256]{2,1,0:T(8,128)(2,1)S(1)} async-done(((bf16[64,8,256]{2,1,0:T(8,128)(2,1)}), bf16[64,8,256]{2,1,0:T(8,128)(2,1)S(1)}, u32[]{:S(2)}, u32[]{:S(2)}) %all-to-all-start) | async-done | bytes 262176 | tf_op jit(solution)/shard_map/all_to_all | solution.py:284
  71.8 30.5 %conv.1 = (bf16[64,8,256]{2,1,0:T(8,128)(2,1)S(1)}, f32[128,128]{1,0:T(8,128)S(1)}) custom-call(bf16[64,8,256]{2,1,0:T(8,128)(2,1)S(1)} %all-to-all-done.x_ref, f32[128,128]{1,0:T(8,128)S(1)} %bitcast.72), custom_call_target="tpu_custom_call" | custom-call | tf_op jit(solution)/shard_map/conv/pallas_call | solution.py:125
  102.3 16.3 %all_to_all.26 = bf16[64,8,256]{2,1,0:T(8,128)(2,1)S(1)} all-to-all(bf16[64,8,256]{2,1,0:T(8,128)(2,1)S(1)} %get-tuple-element.9), channel_id=1, replica_groups=mesh['ctx'=64,'tp'=4,'dp'=2] {'ctx'}, dimensions={0} | all-to-all | bytes 524288 | tf_op jit(solution)/shard_map/all_to_all | solution.py:286
  118.6 0.1 fusion.13
  118.6 0.7 reshape.78
  119.3 1.0 copy.31
  120.3 1.3 rev.10
  121.7 0.8 reshape.87
  122.5 1.8 copy.30
  124.3 1.9 fusion.8
  126.2 1.3 fusion.15
  127.5 0.0 reduce-scatter.2.cloned.1.call-update
  127.5 0.8 reduce.1
  128.4 0.0 copy-start.2
  128.4 14.8 %all_to_all.27 = bf16[64,2,128]{2,1,0:T(2,128)(2,1)S(1)} all-to-all(bf16[64,2,128]{2,1,0:T(2,128)(2,1)S(1)} %reshape.91), channel_id=1, replica_groups=mesh['ctx'=64,'tp'=4,'dp'=2] {'ctx'}, dimensions={0} | all-to-all | bytes 65536 | tf_op jit(solution)/shard_map/all_to_all | solution.py:287
  143.2 0.1 convert_element_type.87
  143.3 0.1 rev.11
  143.4 11.6 %psum.7 = f32[16,256]{1,0:T(8,128)S(1)} all-reduce(f32[16,256]{1,0:T(8,128)S(1)} %bitcast.80), channel_id=1, replica_groups=mesh['ctx'=64,'tp'=4,'dp'=2] {'dp'}, use_global_device_ids=true, to_apply=%region_5.6 | all-reduce | flops 4096 | bytes 32768 | tf_op jit(solution)/shard_map/psum | solution.py:302
  155.0 0.6 broadcast_multiply_fusion.1
  155.6 0.5 multiply_reduce_fusion.2
  156.1 0.1 broadcast_multiply_fusion
  156.2 1.3 collective-permute-start.2
  157.5 1.0 pad_add_fusion
  158.6 0.3 fusion.3.part_ref
  159.0 32.5 %reduce_all.1 = (f32[256,1024]{1,0:T(8,128)S(1)}, f32[16,256]{1,0:T(8,128)S(1)}) custom-call(f32[256,1024]{1,0:T(8,128)S(1)} %fusion.3.part_ref, f32[16,256]{1,0:T(8,128)S(1)} %concatenate.19.small_ref), custom_call_target="tpu_custom_call" | custom-call | tf_op jit(solution)/shard_map/reduce_all/pallas_call | solution.py:248
  191.5 0.6 reshape.83
  192.1 0.0 collective-permute-done.2
  192.1 0.8 fusion.7
  192.9 1.6 convert_bitcast_fusion
  194.5 1.0 copy.45
  (29 shorter events, 0.3 us)
Async XLA Ops:
  7.2 37.7 %copy-start = (bf16[256,1024]{1,0:T(8,128)(2,1)S(1)}, bf16[256,1024]{1,0:T(8,128)(2,1)}, u32[]{:S(2)}) copy-start(bf16[256,1024]{1,0:T(8,128)(2,1)} %param.10) | copy-start | bytes 1572868
  8.0 37.3 %collective-permute-start.1 = (s32[2]{0:T(128)S(1)}, s32[2]{0:T(128)S(1)}, u32[]{:S(2)}, u32[]{:S(2)}) collective-permute-start(s32[2]{0:T(128)S(1)} %slice_bitcast_fusion.3), channel_id=1, source_target_pairs={{0,8},{8,16},{16,24},{24,32},{32,40},{40,48},{48,56},{56,64},{64,7... | collective-permute-start | bytes 32 | tf_op jit(solution)/shard_map/ppermute | solution.py:19
  12.7 33.3 %collective-permute-start = (bf16[3,2,256]{2,1,0:T(2,128)(2,1)S(1)}, bf16[3,2,256]{2,1,0:T(2,128)(2,1)S(1)}, u32[]{:S(2)}, u32[]{:S(2)}) collective-permute-start(bf16[3,2,256]{2,1,0:T(2,128)(2,1)S(1)} %slice.78), channel_id=1, source_target_pairs={{0,8},{8,16},{16,24},{24,32},{32,40},{40,48},{48,56},{56,64},{64,7... | collective-permute-start | bytes 9224 | tf_op jit(solution)/shard_map/ppermute | solution.py:19
  16.7 16.7 %copy-start.5 = (bf16[1,256,256]{2,1,0:T(8,128)(2,1)S(1)}, bf16[1,256,256]{2,1,0:T(8,128)(2,1)}, u32[]{:S(2)}) copy-start(bf16[1,256,256]{2,1,0:T(8,128)(2,1)} %param.11) | copy-start | bytes 393220
  18.7 14.7 %copy-start.6 = (f32[3,3,256]{2,1,0:T(4,128)S(1)}, f32[3,3,256]{2,1,0:T(4,128)}, u32[]{:S(2)}) copy-start(f32[3,3,256]{2,1,0:T(4,128)} %param.8) | copy-start | bytes 27652
  18.7 29.2 %all-to-all-start.1 = ((bf16[64,2,128]{2,1,0:T(2,128)(2,1)}), bf16[64,2,128]{2,1,0:T(2,128)(2,1)S(1)}, u32[]{:S(2)}, u32[]{:S(2)}) async-start(bf16[64,2,128]{2,1,0:T(2,128)(2,1)} %reshape.89), calls=%async_computation.1 | async-start | bytes 65536 | tf_op jit(solution)/shard_map/all_to_all | solution.py:274
  44.9 1.2 copy-start.4
  45.2 0.7 copy-start.7
  47.9 23.9 %all-to-all-start = ((bf16[64,8,256]{2,1,0:T(8,128)(2,1)}), bf16[64,8,256]{2,1,0:T(8,128)(2,1)S(1)}, u32[]{:S(2)}, u32[]{:S(2)}) async-start(bf16[64,8,256]{2,1,0:T(8,128)(2,1)} %pad_maximum_fusion.1), calls=%async_computation | async-start | bytes 524288 | tf_op jit(solution)/shard_map/all_to_all | solution.py:284
  59.3 133.6 %reduce-scatter.2.cloned.1.call-start = ((), (), s32[]{:S(2)}) async-start(), calls=%async_computation.5 | async-start | bytes 1310720 | tf_op jit(solution)/shard_map/reduce_scatter | solution.py:293
  128.3 27.3 %copy-start.3 = (f32[1,256,256]{2,1,0:T(8,128)S(1)}, f32[1,256,256]{2,1,0:T(8,128)}, u32[]{:S(2)}) copy-start(f32[1,256,256]{2,1,0:T(8,128)} %get-tuple-element.43) | copy-start | bytes 786436
  128.4 27.3 %copy-start.2 = (f32[1,256,256]{2,1,0:T(8,128)S(1)}, f32[1,256,256]{2,1,0:T(8,128)}, u32[]{:S(2)}) copy-start(f32[1,256,256]{2,1,0:T(8,128)} %get-tuple-element.37) | copy-start | bytes 786436
  156.2 35.8 %collective-permute-start.2 = (f32[3,2,256]{2,1,0:T(2,128)S(1)}, f32[3,2,256]{2,1,0:T(2,128)S(1)}, u32[]{:S(2)}, u32[]{:S(2)}) collective-permute-start(f32[3,2,256]{2,1,0:T(2,128)S(1)} %pad_add_fusion.2), channel_id=1, source_target_pairs={{8,0},{16,8},{24,16},{32,24},{40,32},{48,40},{56,48},{64,56},{72,6... | collective-permute-start | bytes 18440 | tf_op jit(solution)/shard_map/ppermute | solution.py:19
  158.9 33.2 %copy-start.1 = (f32[3,258,256]{2,1,0:T(8,128)S(1)}, f32[3,258,256]{2,1,0:T(8,128)}, u32[]{:S(2)}) copy-start(f32[3,258,256]{2,1,0:T(8,128)} %pad_add_fusion) | copy-start | bytes 2377732
Sparse Core Ops, SparseCore 0:
  127.6 24.9 reduce-scatter.1

commit v2 on v0

v2 whole, which is shorter than its diff:
```python
import functools
import math

import jax
import jax.numpy as jnp
from jax import lax
from jax.experimental import pallas as pl
from jax.experimental.pallas import tpu as pltpu
from jax.sharding import PartitionSpec as P

F32 = jnp.float32
BF = jnp.bfloat16
MESH = pl.DeviceIdType.MESH
CTX = 64
TP = 4
TAPS = 3
ROWS = 256
COLS = 256
HALF = 128


def iota(shape, axis):
    return lax.broadcasted_iota(jnp.int32, shape, axis)


def one_hot(condition):
    return jnp.where(condition, 1.0, 0.0).astype(BF)


def across(a, b):
    return lax.dot_general(a, b, (((1,), (1,)), ((), ())), preferred_element_type=F32)


def plain(a, b):
    return jnp.dot(a, b, preferred_element_type=F32)


def layer(
    scale,
    x_ref, seg_ref, taps_ref, filt_ref, w_ref, cot_ref,
    mixed_ref, gin_ref, gtaps_ref, glong_ref, gproj_ref,
    cot_all, halo_out, halo_in, filt_out, filt_in, xe, so, masks, gy,
    send, recv, toep, stacked, acc, gct, gls, lag_out, lag_in,
    ret, back, zbuf, part, mix_out, mix_in,
    pair_out, pair_in, s1, b1_in, s2, b2_in, g2, g1, gp,
    sm0, sm1, sm2, edge_out, edge_in, lag_pair,
    snd, rcv, all_snd, all_rcv,
):
    ctx = lax.axis_index("ctx")
    tp = lax.axis_index("tp")
    dp = lax.axis_index("dp")
    y = lax.rem(ctx, 8)
    z = ctx // 8
    my1 = y * (1 - dp) + z * dp
    my2 = z * (1 - dp) + y * dp
    step1 = 1 + 7 * dp
    step2 = 8 - 7 * dp
    base1 = ctx - my1 * step1
    base2 = ctx - my2 * step2
    other = 1 - dp

    def peer1(k):
        return lax.rem(my1 + k, 8)

    def dev1(k):
        return {"ctx": base1 + peer1(k) * step1}

    def peer2(k):
        return lax.rem(my2 + k, 8)

    def dev2(k):
        return {"ctx": base2 + peer2(k) * step2}

    def peer_tp(k):
        return lax.rem(tp + k, TP)

    def peer_ctx(k):
        return lax.rem(ctx + k, CTX)

    def copy(src, dst, n, dev):
        return pltpu.make_async_remote_copy(
            src, dst, snd.at[n], rcv.at[n], device_id=dev, device_id_type=MESH
        )

    barrier = pltpu.get_barrier_semaphore()

    def greet(k, carry):
        pl.semaphore_signal(barrier, 1, device_id={"ctx": peer_ctx(k)}, device_id_type=MESH)
        return carry

    for k in range(1, TP):
        pl.semaphore_signal(barrier, 1, device_id={"tp": peer_tp(k)}, device_id_type=MESH)
    pl.semaphore_signal(barrier, 1, device_id={"dp": other}, device_id_type=MESH)
    lax.fori_loop(1, CTX, greet, 0)

    rows128 = iota((HALF, HALF), 0)
    cols128 = iota((HALF, HALF), 1)
    flip128 = one_hot(rows128 + cols128 == HALF - 1)
    filt = filt_ref[...].astype(BF)
    filt_out[...] = jnp.concatenate(
        [plain(filt[:, :HALF], flip128), plain(filt[:, HALF:], flip128)], axis=1
    ).reshape(16, 1, COLS)
    seg_row = seg_ref[...].astype(F32)
    seg_col = jnp.transpose(jnp.broadcast_to(seg_row, (HALF, ROWS)))
    halo_out[0:6, :] = jnp.concatenate([x_ref[i, ROWS - 2 : ROWS, :].astype(F32) for i in range(3)], axis=0)
    halo_out[6:8, :] = jnp.concatenate([seg_col[ROWS - 2 : ROWS, :]] * 2, axis=1)
    pl.semaphore_wait(barrier, CTX - 1 + TP - 1 + 1)

    halo = copy(halo_out, halo_in, 0, {"ctx": peer_ctx(1)})
    halo.start()
    cot_copies = []
    for k in range(1, TP):
        c = copy(cot_ref, cot_all.at[tp], k, {"tp": peer_tp(k)})
        c.start()
        cot_copies.append(c)

    def send_filter(k, carry):
        peer = peer_ctx(k)
        pltpu.make_async_remote_copy(
            filt_out.at[peer // 4], filt_in.at[ctx], all_snd.at[0], all_rcv.at[0],
            device_id={"ctx": peer}, device_id_type=MESH,
        ).start()
        return carry

    lax.fori_loop(1, CTX, send_filter, 0)
    filt_in[pl.ds(ctx, 1)] = filt_out[pl.ds(ctx // 4, 1)]
    cot_all[pl.ds(tp, 1)] = cot_ref[...].reshape(1, ROWS, COLS)

    def wait_all(buf, n, which):
        pltpu.make_async_copy(buf.at[pl.ds(0, CTX - 1)], buf.at[pl.ds(0, CTX - 1)], which.at[n]).wait()

    for i in range(3):
        xe[i, 8 : 8 + ROWS, :] = x_ref[i].astype(F32)
    halo.wait()

    for i in range(3):
        xe[i, 6:8, :] = halo_in[2 * i : 2 * i + 2, :]
    prev_seg = jnp.where(ctx == 0, -1.0, halo_in[6:8, 0:HALF])
    before1 = jnp.concatenate([prev_seg[1:2], seg_col[: ROWS - 1]], axis=0)
    before2 = jnp.concatenate([prev_seg, seg_col[: ROWS - 2]], axis=0)
    for n, before in enumerate((before1, before2)):
        mask = jnp.where(before == seg_col, 1.0, 0.0)
        masks[n] = jnp.concatenate([mask, mask], axis=1)
    for i in range(3):
        so[i] = (
            taps_ref[i, 0:1, :] * xe[i, 8 : 8 + ROWS, :]
            + taps_ref[i, 1:2, :] * masks[0] * xe[i, 7 : 7 + ROWS, :]
            + taps_ref[i, 2:3, :] * masks[1] * xe[i, 6 : 6 + ROWS, :]
        )

    wait_all(filt_in, 0, all_rcv)
    keep = rows128 >= cols128

    def spread(line):
        return pltpu.roll(jnp.broadcast_to(line, (HALF, HALF)), 1, 1, stride=1, stride_axis=0)

    def build(n, prev):
        for u in range(2):
            d = 2 * n + u
            line = filt_in[d]
            s0 = spread(line[:, :HALF])
            a0 = jnp.where(keep, s0, prev).astype(BF)
            s1_ = spread(line[:, HALF:])
            a1 = jnp.where(keep, s1_, s0).astype(BF)
            base = pl.multiple_of(d * 256, 256)
            toep[pl.ds(base, HALF), 0:HALF] = a0
            toep[pl.ds(base + HALF, HALF), HALF:COLS] = a0
            toep[pl.ds(base + HALF, HALF), 0:HALF] = a1
            toep[pl.ds(base + 256, HALF), HALF:COLS] = a1
            prev = s1_
        return prev

    toep[0:HALF, HALF:COLS] = jnp.zeros((HALF, HALF), BF)
    lax.fori_loop(0, 32, build, jnp.zeros((HALF, HALF), F32))

    for c in cot_copies:
        c.wait()
    total = across(cot_all[0], w_ref[:, 0:256])
    for i in range(1, TP):
        total += across(cot_all[i], w_ref[:, 256 * i : 256 * i + 256])
    gy[...] = total
    flip = one_hot(iota((ROWS, ROWS), 0) + iota((ROWS, ROWS), 1) == ROWS - 1)
    slot = iota((512, COLS), 0)
    chan = iota((512, COLS), 1)
    home = (slot // 8) * 4 + lax.rem(slot, 8)
    pick_a = one_hot((home == chan) & (lax.rem(slot, 8) < 4))
    pick_b = one_hot((home == chan + 4) & (lax.rem(slot, 8) >= 4))
    gated = (so[1] * so[2]).astype(BF)
    gated_back = plain(flip, gated).astype(BF)
    glo = (total * so[0]).astype(BF)
    send[...] = (across(pick_a, gated_back) + across(pick_b, glo)).reshape(CTX, 8, ROWS).astype(BF)

    def scatter(src, dst, n):
        def one(k, carry):
            peer = peer_ctx(k)
            pltpu.make_async_remote_copy(
                src.at[peer], dst.at[ctx], all_snd.at[n], all_rcv.at[n],
                device_id={"ctx": peer}, device_id_type=MESH,
            ).start()
            return carry

        lax.fori_loop(1, CTX, one, 0)
        dst[pl.ds(ctx, 1)] = src[pl.ds(ctx, 1)]

    scatter(send, recv, 1)
    wait_all(recv, 1, all_rcv)

    x8 = recv[...].astype(F32)
    first = iota((8, COLS), 0) < 4
    joined = jnp.concatenate([jnp.where(first, x8[k], x8[CTX - 1 - k]) for k in range(CTX)], axis=0)
    for e in range(4):
        if e:
            stacked[:, 256 * e : 256 * e + 256] = jnp.concatenate(
                [jnp.zeros((8 * e, COLS), F32), joined[: 512 - 8 * e]], axis=0
            ).astype(BF)
        else:
            stacked[:, 0:256] = joined.astype(BF)
    for n in range(16):
        term = plain(stacked[0 : 512 - 32 * n, :], toep[1024 * n : 1024 * n + 1024, :])
        if n:
            acc[32 * n : 512, :] += term
        else:
            acc[...] = term
    for k in range(CTX):
        ret[k] = jnp.where(first, acc[8 * k : 8 * k + 8, :], acc[504 - 8 * k : 512 - 8 * k, :]).astype(BF)
    scatter(ret, back, 2)

    pairs = recv[...].astype(F32).reshape(32, 16, COLS)
    even = pairs[:, 0:8]
    odd = pairs[:, 8:16]
    even_r = pltpu.roll(even, 4, 1)
    odd_r = pltpu.roll(odd, 4, 1)
    first3 = iota((32, 8, COLS), 1) < 4
    gct[...] = jnp.transpose(jnp.where(first3, even, odd_r).reshape(256, COLS)).astype(BF)
    straight = jnp.where(first3, even_r, odd).reshape(256, COLS)
    next_even = jnp.concatenate([even[1:], jnp.zeros((1, 8, COLS), F32)], axis=0)
    next_even = jnp.where(iota((32, 8, COLS), 0) < 31, next_even, 0.0)
    crossed = jnp.where(first3, odd_r, next_even).reshape(256, COLS)
    zero8 = jnp.zeros((8, COLS), F32)
    for n, value in enumerate(
        (straight, crossed, jnp.concatenate([straight[8:], zero8], axis=0), jnp.concatenate([crossed[8:], zero8], axis=0))
    ):
        gls[n, 0:256, :] = value.astype(BF)
        gls[n, 256:512, :] = jnp.zeros((256, COLS), BF)
    later = cols128 > rows128

    def roll_up(block):
        return pltpu.roll(block, 1, 1, stride=1, stride_axis=0)

    def lag_row(now, last):
        return jnp.sum(jnp.where(later, now, last), axis=0, keepdims=True).reshape(1, 1, HALF)

    def correlate(width):
        def body(m, carry):
            c11, last = carry
            for u in range(4):
                c = plain(gct[:, 0:width], gls[u, pl.ds(pl.multiple_of(16 * m, 16), width), :])
                r0 = roll_up(c11 + c[:HALF, :HALF])
                r1 = roll_up(c[:HALF, HALF:] + c[HALF:, :HALF])
                lag_out[pl.ds(8 * m + 2 * u, 1)] = lag_row(r0, last)
                lag_out[pl.ds(8 * m + 2 * u + 1, 1)] = lag_row(r1, r0)
                c11 = c[HALF:, HALF:]
                last = r1
            return c11, last

        return body

    nothing = jnp.zeros((HALF, HALF), F32)
    carry = lax.fori_loop(0, 8, correlate(256), (nothing, nothing))
    c11, last = lax.fori_loop(8, 16, correlate(128), carry)
    r0 = roll_up(c11)
    lag_out[128:129] = lag_row(r0, last)
    lag_out[129:130] = lag_row(nothing, r0)

    def send_lags(k, carry):
        peer = peer_ctx(k)
        pltpu.make_async_remote_copy(
            lag_out.at[pl.ds(2 * peer + 2, 2)], lag_in.at[ctx], all_snd.at[3], all_rcv.at[3],
            device_id={"ctx": peer}, device_id_type=MESH,
        ).start()
        return carry

    lax.fori_loop(1, CTX, send_lags, 0)
    lag_in[pl.ds(ctx, 1)] = lag_out[pl.ds(2 * ctx + 2, 2)].reshape(1, 2, 1, HALF)

    wait_all(back, 2, all_rcv)
    got = back[...].astype(F32).reshape(512, ROWS).astype(BF)
    slot_t = iota((COLS, 512), 1)
    chan_t = iota((COLS, 512), 0)
    home_t = (slot_t // 8) * 4 + lax.rem(slot_t, 8)
    take_a = one_hot((home_t == chan_t) & (lax.rem(slot_t, 8) < 4))
    take_b = one_hot((home_t == chan_t + 4) & (lax.rem(slot_t, 8) >= 4))
    same = one_hot(iota((ROWS, ROWS), 0) == iota((ROWS, ROWS), 1))
    long_out = across(flip, plain(take_a, got).astype(BF))
    grad_gated = across(same, plain(take_b, got).astype(BF))
    y_all = so[0] * long_out
    y_hi = y_all.astype(BF)
    y_lo = (y_all - y_hi.astype(F32)).astype(BF)
    y_hi_t = across(same, y_hi).astype(BF)
    y_lo_t = across(same, y_lo).astype(BF)
    for i in range(TP):
        part[:, 256 * i : 256 * i + 256] = plain(y_hi_t, cot_all[i]) + plain(y_lo_t, cot_all[i])
    off = pl.multiple_of(other * HALF, HALF)
    mine = pl.multiple_of(dp * HALF, HALF)
    pair_out[...] = part[pl.ds(off, HALF), :].astype(BF)
    pair_copy = copy(pair_out, pair_in, 4, {"dp": other})
    pair_copy.start()
    for i in range(TP):
        mix_out[i] = (plain(y_hi, w_ref[:, 256 * i : 256 * i + 256]) + plain(y_lo, w_ref[:, 256 * i : 256 * i + 256])).astype(BF)
    mix_copies = []
    for k in range(1, TP):
        c = copy(mix_out.at[peer_tp(k)], mix_in.at[tp], 4 + k, {"tp": peer_tp(k)})
        c.start()
        mix_copies.append(c)

    def rows16(k):
        return pl.ds(pl.multiple_of(k * 16, 16), 16)

    def cols_of(k):
        return pl.ds(pl.multiple_of(k * HALF, HALF), HALF)

    pair_copy.wait()
    s1[...] = (part[pl.ds(mine, HALF), :] + pair_in[...].astype(F32)).astype(BF)
    first_copies = []
    for k in range(1, 8):
        c = copy(s1.at[rows16(peer1(k)), :], b1_in.at[k], 7 + k, dev1(k))
        c.start()
        first_copies.append(c)

    gso = [gy[...] * long_out, grad_gated * so[2], grad_gated * so[1]]
    edge_out[6:8, :] = jnp.zeros((2, COLS), F32)
    sm0[0, 9:16, :] = jnp.zeros((7, COLS), F32)
    for i in range(3):
        z1 = gso[i] * masks[0]
        z2 = gso[i] * masks[1]
        f0, f1, f2 = (taps_ref[i, s : s + 1, :] for s in range(TAPS))
        edge_out[2 * i : 2 * i + 1, :] = f2 * z2[0:1]
        edge_out[2 * i + 1 : 2 * i + 2, :] = f1 * z1[0:1] + f2 * z2[1:2]
        zbuf[0, 0:ROWS, :] = z1
        zbuf[1, 0:ROWS, :] = z2
        zbuf[:, ROWS : ROWS + 8, :] = jnp.zeros((2, 8, COLS), F32)
        sm0[0, 3 * i : 3 * i + 1, :] = jnp.sum(gso[i] * xe[i, 8 : 8 + ROWS, :], axis=0, keepdims=True)
        sm0[0, 3 * i + 1 : 3 * i + 2, :] = jnp.sum(z1 * xe[i, 7 : 7 + ROWS, :], axis=0, keepdims=True)
        sm0[0, 3 * i + 2 : 3 * i + 3, :] = jnp.sum(z2 * xe[i, 6 : 6 + ROWS, :], axis=0, keepdims=True)
        xe[i, 0:ROWS, :] = f0 * gso[i] + f1 * zbuf[0, 1 : 1 + ROWS, :] + f2 * zbuf[1, 2 : 2 + ROWS, :]
    edge_copy = copy(edge_out, edge_in, 15, {"ctx": peer_ctx(CTX - 1)})
    edge_copy.start()
    small_pair = copy(sm0.at[0], sm0.at[1], 16, {"dp": other})
    small_pair.start()

    for c in first_copies:
        c.wait()
    total = s1[rows16(my1), :].astype(F32)
    for k in range(1, 8):
        total += b1_in[k].astype(F32)
    s2[...] = total
    second_copies = []
    for k in range(1, 8):
        c = copy(s2.at[:, cols_of(peer2(k))], b2_in.at[k], 16 + k, dev2(k))
        c.start()
        second_copies.append(c)
    small_pair.wait()
    sm1[0] = sm0[0] + sm0[1]
    small_first = []
    for k in range(1, 8):
        c = copy(sm1.at[0], sm1.at[k], 23 + k, dev1(k))
        c.start()
        small_first.append(c)

    wait_all(lag_in, 3, all_rcv)
    for g in range(16):
        for h in range(2):
            value = lag_in[4 * g, h] + lag_in[4 * g + 1, h] + lag_in[4 * g + 2, h] + lag_in[4 * g + 3, h]
            lag_pair[0, g : g + 1, HALF * h : HALF * h + HALF] = value
    lag_copy = copy(lag_pair.at[0], lag_pair.at[1], 31, {"dp": other})
    lag_copy.start()

    for c in second_copies:
        c.wait()
    total = s2[:, cols_of(my2)]
    for k in range(1, 8):
        total += b2_in[k]
    g2[:, cols_of(my2)] = (total * scale).astype(BF)
    third_copies = []
    for k in range(1, 8):
        c = copy(g2.at[:, cols_of(my2)], g2.at[:, cols_of(my2)], 31 + k, dev2(k))
        c.start()
        third_copies.append(c)
    for c in small_first:
        c.wait()
    small = sm1[0]
    for k in range(1, 8):
        small += sm1[k]
    sm2[0] = small
    small_second = []
    for k in range(1, 8):
        c = copy(sm2.at[0], sm2.at[k], 38 + k, dev2(k))
        c.start()
        small_second.append(c)
    edge_copy.wait()
    for i in range(3):
        xe[i, ROWS - 2 : ROWS, :] += edge_in[2 * i : 2 * i + 2, :]
        gin_ref[i] = xe[i, 0:ROWS, :].astype(BF)

    for c in third_copies:
        c.wait()
    g1[rows16(my1), :] = g2[...]
    fourth_copies = []
    for k in range(1, 8):
        c = copy(g1.at[rows16(my1), :], g1.at[rows16(my1), :], 45 + k, dev1(k))
        c.start()
        fourth_copies.append(c)
    for c in mix_copies:
        c.wait()
    total = mix_out[pl.ds(tp, 1)].astype(F32)
    for k in range(1, TP):
        total += mix_in[pl.ds(peer_tp(k), 1)].astype(F32)
    mixed_ref[...] = total.reshape(ROWS, COLS).astype(BF)
    lag_copy.wait()
    glong_ref[...] = (lag_pair[0] + lag_pair[1]) * scale
    for c in small_second:
        c.wait()
    small = sm2[0]
    for k in range(1, 8):
        small += sm2[k]
    gtaps_ref[...] = small * scale
    for n in range(3):
        buf = (filt_in, send, ret)[n]
        wait_all(buf, n, all_snd)
    pltpu.make_async_copy(lag_in.at[pl.ds(0, CTX - 1)], lag_in.at[pl.ds(0, CTX - 1)], all_snd.at[3]).wait()
    for c in fourth_copies:
        c.wait()
    last_copy = copy(g1, gp, 53, {"dp": other})
    last_copy.start()
    gproj_ref[pl.ds(mine, HALF), :] = g1[...]
    last_copy.wait()
    gproj_ref[pl.ds(off, HALF), :] = gp[...]


def per_device(projected, segment_ids, short_filter, long_filter, out_proj, mixed_cotangent):
    scale = 1.0 / math.sqrt(2 * ROWS * CTX)
    V = pltpu.VMEM
    spec = pl.BlockSpec(memory_space=pltpu.VMEM)
    mixed, grad_in, grad_taps, grad_long, grad_proj = pl.pallas_call(
        functools.partial(layer, scale),
        out_shape=(
            jax.ShapeDtypeStruct((ROWS, COLS), BF),
            jax.ShapeDtypeStruct((3, ROWS, COLS), BF),
            jax.ShapeDtypeStruct((16, COLS), F32),
            jax.ShapeDtypeStruct((16, COLS), F32),
            jax.ShapeDtypeStruct((256, 1024), BF),
        ),
        in_specs=[spec] * 6,
        out_specs=[spec] * 5,
        scratch_shapes=[
            V((TP, ROWS, COLS), BF), V((8, COLS), F32), V((8, COLS), F32),
            V((16, 1, COLS), F32), V((CTX, 1, COLS), F32),
            V((3, ROWS + 8, COLS), F32), V((3, ROWS, COLS), F32), V((2, ROWS, COLS), F32), V((ROWS, COLS), F32),
            V((CTX, 8, ROWS), BF), V((CTX, 8, ROWS), BF),
            V((64 * 256 + 256, 256), BF), V((512, 1024), BF), V((512, 256), F32),
            V((256, 256), BF), V((4, 512, 256), BF), V((130, 1, HALF), F32), V((CTX, 2, 1, HALF), F32),
            V((CTX, 8, ROWS), BF), V((CTX, 8, ROWS), BF),
            V((2, ROWS + 8, COLS), F32), V((256, 1024), F32), V((TP, ROWS, COLS), BF), V((TP, ROWS, COLS), BF),
            V((HALF, 1024), BF), V((HALF, 1024), BF), V((HALF, 1024), BF), V((8, 16, 1024), BF),
            V((16, 1024), F32), V((8, 16, HALF), F32), V((16, 1024), BF), V((HALF, 1024), BF), V((HALF, 1024), BF),
            V((2, 16, COLS), F32), V((8, 16, COLS), F32), V((8, 16, COLS), F32),
            V((8, COLS), F32), V((8, COLS), F32), V((2, 16, COLS), F32),
            pltpu.SemaphoreType.DMA((54,)), pltpu.SemaphoreType.DMA((54,)),
            pltpu.SemaphoreType.DMA((4,)), pltpu.SemaphoreType.DMA((4,)),
        ],
        compiler_params=pltpu.CompilerParams(vmem_limit_bytes=48 << 20, collective_id=0, has_side_effects=True),
        name="layer",
    )(projected[:, 0], segment_ids, short_filter, long_filter, out_proj, mixed_cotangent[0])
    return (
        mixed[None],
        grad_in[:, None],
        grad_taps[:9].reshape(3, 3, COLS),
        grad_long,
        grad_proj.astype(F32),
    )


def solution(mesh):
    in_specs = (
        P(None, "dp", "ctx", "tp"),
        P("dp", "ctx"),
        P(None, None, "tp"),
        P("tp", "ctx"),
        P("tp", None),
        P("dp", "ctx", "tp"),
    )
    out_specs = (
        P("dp", "ctx", "tp"),
        P(None, "dp", "ctx", "tp"),
        P(None, None, "tp"),
        P("tp", "ctx"),
        P("tp", None),
    )
    return jax.shard_map(
        per_device, mesh=mesh, in_specs=in_specs, out_specs=out_specs, check_vma=False
    )
```

time: 870 us -> 87.6 us (0.10); the launches traced: 855 us -> 87.2 us
  blocking collectives: 522 us -> 0 us
  waiting for transfers between devices: 122 us -> 0 us
  starting transfers between devices: 88.1 us -> 0 us
  Pallas kernels: 0 us -> 77.8 us
  matrix products: 44.2 us -> 0 us
  local copies, waits for them, and re-layouts: 45.5 us -> 7.65 us
  between operations: 16.7 us -> 0.66 us
  other arithmetic: 16.9 us -> 1.09 us
    psum x2 -> x0, blocking collectives: 511 us -> none  [the longest x1 501 us: per_device(): lax.psum((grad_proj_local, grad_short_local), ('ctx', 'dp'))]
    all_to_all x12 -> x0, waiting for transfers between devices: 121 us -> none  [the longest x2 28.4 us: inverse_spectrum(): lax.all_to_all(twist_re, 'ctx', split_axis=1, concat_axis=0, tiled=True)]
    all_to_all x12 -> x0, starting transfers between devices: 79.4 us -> none  [the longest x2 19.3 us: forward_spectrum(): lax.all_to_all(real_part[None], 'ctx', split_axis=1, concat_axis=0, tiled...]
    pallas_call x0 -> x1, Pallas kernels: none -> 77.8 us  [per_device(): pl.pallas_call(functools.partial(layer, scale), out_shape=(jax.ShapeDtype...]
    dot_general x27 -> x0, matrix products: 44.2 us -> none  [the longest x16 34.1 us: along_rows(): jnp.einsum('kmc,mq->kqc', blocks, matrix, precision=highest_precision)]
    all_to_all x12 -> x0, local copies, waits for them, and re-layouts: 13.8 us -> none  [the longest x3 5.62 us: inverse_spectrum(): lax.all_to_all(twist_im, 'ctx', split_axis=1, concat_axis=0, tiled=True)]
    all_gather x1 -> x0, blocking collectives: 11.7 us -> none  [per_device(): cot_full = lax.all_gather(mixed_cotangent[0], 'tp', axis=1, tiled=True)]
  transfers between devices with their start and end apart: 17 -> 0, of which waited for: 12 -> 0; matrix products, arithmetic and copies ran while one was open for 7% -> 0% of each run, Pallas kernels for 0% -> 0%
where the time goes in v2:
time: 87.6 us; the launch traced here: 87.2 us
  Pallas kernels  77.8 us (89%)
  local copies, waits for them, and re-layouts  7.65 us (9%)
  other arithmetic  1.09 us (1%)
    pallas_call x1, Pallas kernels, per_device(): pl.pallas_call(functools.partial(layer, scale), out_shape=(jax.ShapeDtype...  77.8 us
    unnamed x15, local copies, waits for them, and re-layouts  7.04 us

profile of v2, /device:TPU:1, one launch (start us, length us, event | category | flops | bytes accessed | tf_op | source)
XLA Modules:
  0.0 87.2 jit_solution(1030037236469680617)
XLA Ops:
  0.6 0.0 copy-start.5
  0.6 0.7 copy-done.5
  1.3 0.0 copy-start
  1.3 1.0 %copy-done = bf16[256,1024]{1,0:T(8,128)(2,1)S(1)} copy-done((bf16[256,1024]{1,0:T(8,128)(2,1)S(1)}, bf16[256,1024]{1,0:T(8,128)(2,1)}, u32[]{:S(2)}) %copy-start) | copy-done | bytes 524312
  2.4 0.0 copy-start.1
  2.4 1.0 %copy-done.1 = bf16[3,1,256,256]{3,2,1,0:T(8,128)(2,1)S(1)} copy-done((bf16[3,1,256,256]{3,2,1,0:T(8,128)(2,1)S(1)}, bf16[3,1,256,256]{3,2,1,0:T(8,128)(2,1)}, u32[]{:S(2)}) %copy-start.1) | copy-done | bytes 393240
  3.4 0.0 copy-start.2
  3.4 0.9 %copy-done.2 = bf16[1,256,256]{2,1,0:T(8,128)(2,1)S(1)} copy-done((bf16[1,256,256]{2,1,0:T(8,128)(2,1)S(1)}, bf16[1,256,256]{2,1,0:T(8,128)(2,1)}, u32[]{:S(2)}) %copy-start.2) | copy-done | bytes 131096
  4.3 0.0 copy-start.3
  4.3 0.7 copy-done.3
  5.0 0.0 copy-start.4
  5.0 0.7 copy-done.4
  5.7 77.8 %layer.1 = (bf16[256,256]{1,0:T(8,128)(2,1)S(1)}, bf16[3,256,256]{2,1,0:T(8,128)(2,1)S(1)}, f32[16,256]{1,0:T(8,128)S(1)}, f32[16,256]{1,0:T(8,128)S(1)}, bf16[256,1024]{1,0:T(8,128)(2,1)S(1)}) custom-call(bf16[3,256,256]{2,1,0:T(8,128)(2,1)S(1)} %bitcast.7, s32[1,256]{1,0:T(1,128)S(1)} %copy-done.5, f32[3,3,256]{2,1,0:T(4,128)S(1)} %copy-done.4, ...), custom_call_target="tpu_custom_call" | custom-call | tf_op jit(solution)/shard_map/layer/pallas_call | solution.py:444
  83.5 0.6 reshape.13
  84.1 1.1 %convert_element_type.3 = f32[256,1024]{1,0:T(8,128)} convert(bf16[256,1024]{1,0:T(8,128)(2,1)S(1)} %get-tuple-element.14) | non-fusion elementwise | flops 262144 | bytes 1572864 | tf_op jit(solution)/shard_map/convert_element_type | solution.py:479
  85.2 0.7 copy.15
  85.9 0.7 copy.16
  86.6 0.6 copy.17
Async XLA Ops:
  0.6 0.7 copy-start.5
  1.3 1.0 %copy-start = (bf16[256,1024]{1,0:T(8,128)(2,1)S(1)}, bf16[256,1024]{1,0:T(8,128)(2,1)}, u32[]{:S(2)}) copy-start(bf16[256,1024]{1,0:T(8,128)(2,1)} %w_ref.1) | copy-start | bytes 1572868
  2.4 1.0 %copy-start.1 = (bf16[3,1,256,256]{3,2,1,0:T(8,128)(2,1)S(1)}, bf16[3,1,256,256]{3,2,1,0:T(8,128)(2,1)}, u32[]{:S(2)}) copy-start(bf16[3,1,256,256]{3,2,1,0:T(8,128)(2,1)} %param.6) | copy-start | bytes 1179652
  3.4 0.9 %copy-start.2 = (bf16[1,256,256]{2,1,0:T(8,128)(2,1)S(1)}, bf16[1,256,256]{2,1,0:T(8,128)(2,1)}, u32[]{:S(2)}) copy-start(bf16[1,256,256]{2,1,0:T(8,128)(2,1)} %param.11) | copy-start | bytes 393220
  4.3 0.7 copy-start.3
  5.0 0.7 copy-start.4

commit v3 on v2

v3 whole, which is shorter than its diff:
```python
import functools
import math

import jax
import jax.numpy as jnp
from jax import lax
from jax.experimental import pallas as pl
from jax.experimental.pallas import tpu as pltpu
from jax.sharding import PartitionSpec as P

F32 = jnp.float32
BF = jnp.bfloat16
MESH = pl.DeviceIdType.MESH
CTX = 64
TP = 4
TAPS = 3
ROWS = 256
COLS = 256
HALF = 128


def iota(shape, axis):
    return lax.broadcasted_iota(jnp.int32, shape, axis)


def one_hot(condition):
    return jnp.where(condition, 1.0, 0.0).astype(BF)


def across(a, b):
    return lax.dot_general(a, b, (((1,), (1,)), ((), ())), preferred_element_type=F32)


def plain(a, b):
    return jnp.dot(a, b, preferred_element_type=F32)


def layer(
    scale,
    x_hbm, seg_hbm, taps_hbm, filt_hbm, w_hbm, cot_hbm,
    mixed_ref, gin_ref, gtaps_ref, glong_ref, gproj_ref,
    x_ref, seg_ref, taps_ref, filt_ref, w_ref, load_sem,
    cot_all, halo_out, halo_in, filt_out, filt_in, xe, so, masks, gy,
    send_g, recv_g, send_l, recv_l, toep, stacked, acc, gct, gls, kept, lag_out, lag_in,
    ret_f, back_f, ret_b, back_b, zbuf, y_t, part, mix_out, mix_in,
    pair_out, pair_in, sum_out, sum_in, one_tile, tiles, tiles_in,
    sm0, sm1, sm2, edge_out, edge_in, lag_pair,
    snd, rcv, all_snd, all_rcv, grp,
):
    ctx = lax.axis_index("ctx")
    tp = lax.axis_index("tp")
    dp = lax.axis_index("dp")
    y = lax.rem(ctx, 8)
    z = ctx // 8
    my1 = y * (1 - dp) + z * dp
    my2 = z * (1 - dp) + y * dp
    step1 = 1 + 7 * dp
    step2 = 8 - 7 * dp
    base1 = ctx - my1 * step1
    base2 = ctx - my2 * step2
    other = 1 - dp

    def peer1(k):
        return lax.rem(my1 + k, 8)

    def dev1(k):
        return {"ctx": base1 + peer1(k) * step1}

    def peer2(k):
        return lax.rem(my2 + k, 8)

    def dev2(k):
        return {"ctx": base2 + peer2(k) * step2}

    def peer_tp(k):
        return lax.rem(tp + k, TP)

    def peer_ctx(k):
        return lax.rem(ctx + k, CTX)

    def copy(src, dst, n, dev):
        return pltpu.make_async_remote_copy(
            src, dst, snd.at[n], rcv.at[n], device_id=dev, device_id_type=MESH
        )

    barrier = pltpu.get_barrier_semaphore()

    def greet(k, carry):
        pl.semaphore_signal(barrier, 1, device_id={"ctx": peer_ctx(k)}, device_id_type=MESH)
        return carry

    for k in range(1, TP):
        pl.semaphore_signal(barrier, 1, device_id={"tp": peer_tp(k)}, device_id_type=MESH)
    pl.semaphore_signal(barrier, 1, device_id={"dp": other}, device_id_type=MESH)
    lax.fori_loop(1, CTX, greet, 0)
    loads = []
    for n, (src, dst) in enumerate((
        (filt_hbm, filt_ref), (seg_hbm, seg_ref), (x_hbm, x_ref),
        (cot_hbm, cot_all.at[tp]), (taps_hbm, taps_ref), (w_hbm, w_ref),
    )):
        load = pltpu.make_async_copy(src, dst, load_sem.at[n])
        load.start()
        loads.append(load)

    for load in loads[:3]:
        load.wait()
    rows128 = iota((HALF, HALF), 0)
    cols128 = iota((HALF, HALF), 1)
    flip128 = one_hot(rows128 + cols128 == HALF - 1)
    filt = filt_ref[...].astype(BF)
    filt_out[...] = jnp.concatenate(
        [plain(filt[:, :HALF], flip128), plain(filt[:, HALF:], flip128)], axis=1
    ).reshape(16, 1, COLS)
    seg_row = seg_ref[...].astype(F32)
    seg_col = jnp.transpose(jnp.broadcast_to(seg_row, (HALF, ROWS)))
    halo_out[0:6, :] = jnp.concatenate([x_ref[i, ROWS - 2 : ROWS, :].astype(F32) for i in range(3)], axis=0)
    halo_out[6:8, :] = jnp.concatenate([seg_col[ROWS - 2 : ROWS, :]] * 2, axis=1)
    loads[3].wait()
    pl.semaphore_wait(barrier, CTX - 1 + TP - 1 + 1)

    halo = copy(halo_out, halo_in, 0, {"ctx": peer_ctx(1)})
    halo.start()
    cot_copies = []
    for k in range(1, TP):
        c = copy(cot_all.at[tp], cot_all.at[tp], k, {"tp": peer_tp(k)})
        c.start()
        cot_copies.append(c)

    def send_filter(k, carry):
        peer = peer_ctx(k)
        pltpu.make_async_remote_copy(
            filt_out.at[peer // 4], filt_in.at[ctx], all_snd.at[0], all_rcv.at[0],
            device_id={"ctx": peer}, device_id_type=MESH,
        ).start()
        return carry

    lax.fori_loop(1, CTX, send_filter, 0)
    filt_in[pl.ds(ctx, 1)] = filt_out[pl.ds(ctx // 4, 1)]

    def wait_all(buf, n, which):
        pltpu.make_async_copy(buf.at[pl.ds(0, CTX - 1)], buf.at[pl.ds(0, CTX - 1)], which.at[n]).wait()

    for i in range(3):
        xe[i, 8 : 8 + ROWS, :] = x_ref[i].astype(F32)
    halo.wait()
    loads[4].wait()
    loads[5].wait()

    for i in range(3):
        xe[i, 6:8, :] = halo_in[2 * i : 2 * i + 2, :]
    prev_seg = jnp.where(ctx == 0, -1.0, halo_in[6:8, 0:HALF])
    before1 = jnp.concatenate([prev_seg[1:2], seg_col[: ROWS - 1]], axis=0)
    before2 = jnp.concatenate([prev_seg, seg_col[: ROWS - 2]], axis=0)
    for n, before in enumerate((before1, before2)):
        mask = jnp.where(before == seg_col, 1.0, 0.0)
        masks[n] = jnp.concatenate([mask, mask], axis=1)

    def featurize(i):
        so[i] = (
            taps_ref[i, 0:1, :] * xe[i, 8 : 8 + ROWS, :]
            + taps_ref[i, 1:2, :] * masks[0] * xe[i, 7 : 7 + ROWS, :]
            + taps_ref[i, 2:3, :] * masks[1] * xe[i, 6 : 6 + ROWS, :]
        )

    featurize(1)
    featurize(2)

    def scatter(src, dst, n):
        def one(k, carry):
            peer = peer_ctx(k)
            pltpu.make_async_remote_copy(
                src.at[peer], dst.at[ctx], all_snd.at[n], all_rcv.at[n],
                device_id={"ctx": peer}, device_id_type=MESH,
            ).start()
            return carry

        lax.fori_loop(1, CTX, one, 0)
        dst[pl.ds(ctx, 1)] = src[pl.ds(ctx, 1)]

    slot = iota((512, COLS), 0)
    chan = iota((512, COLS), 1)
    home = (slot // 8) * 4 + lax.rem(slot, 8)
    pick_a = one_hot((home == chan) & (lax.rem(slot, 8) < 4))
    pick_b = one_hot((home == chan + 4) & (lax.rem(slot, 8) >= 4))
    flip = one_hot(iota((ROWS, ROWS), 0) + iota((ROWS, ROWS), 1) == ROWS - 1)

    def tiles_of(value):
        return (across(pick_a, value[:HALF]) + across(pick_b, value[HALF:])).reshape(CTX, 8, HALF).astype(BF)

    send_g[...] = tiles_of(plain(flip, (so[1] * so[2]).astype(BF)).astype(BF))
    scatter(send_g, recv_g, 1)
    featurize(0)

    wait_all(filt_in, 0, all_rcv)
    keep = rows128 >= cols128

    def spread(line):
        return pltpu.roll(jnp.broadcast_to(line, (HALF, HALF)), 1, 1, stride=1, stride_axis=0)

    def build(n, prev):
        for u in range(2):
            d = 2 * n + u
            line = filt_in[d]
            s0 = spread(line[:, :HALF])
            a0 = jnp.where(keep, s0, prev).astype(BF)
            s1_ = spread(line[:, HALF:])
            a1 = jnp.where(keep, s1_, s0).astype(BF)
            base = pl.multiple_of(d * 256, 256)
            toep[pl.ds(base, HALF), 0:HALF] = a0
            toep[pl.ds(base + HALF, HALF), HALF:COLS] = a0
            toep[pl.ds(base + HALF, HALF), 0:HALF] = a1
            toep[pl.ds(base + 256, HALF), HALF:COLS] = a1
            prev = s1_
        return prev

    toep[0:HALF, HALF:COLS] = jnp.zeros((HALF, HALF), BF)
    lax.fori_loop(0, 32, build, jnp.zeros((HALF, HALF), F32))

    for c in cot_copies:
        c.wait()
    total = across(cot_all[0], w_ref[:, 0:256])
    for i in range(1, TP):
        total += across(cot_all[i], w_ref[:, 256 * i : 256 * i + 256])
    gy[...] = total
    send_l[...] = tiles_of((total * so[0]).astype(BF))
    scatter(send_l, recv_l, 2)

    first3 = iota((32, 8, HALF), 1) < 4

    def swap4(value):
        return pltpu.roll(value, 4, 1)

    def halves(ref):
        both = ref[...].astype(F32).reshape(32, 16, HALF)
        return both[:, 0:8], both[:, 8:16]

    def rows_of(one, two):
        return jnp.concatenate(
            [jnp.where(first3, one, swap4(two)), jnp.where(first3, swap4(one), two)], axis=2
        ).reshape(256, COLS)

    def backwards(value):
        return jnp.concatenate([value[31 - i : 32 - i] for i in range(32)], axis=0)

    def convolve(rows):
        for e in range(4):
            if e:
                stacked[:, 256 * e : 256 * e + 256] = jnp.concatenate(
                    [jnp.zeros((4 * e, COLS), F32), rows[: 256 - 4 * e]], axis=0
                ).astype(BF)
            else:
                stacked[:, 0:256] = rows.astype(BF)
        for n in range(16):
            term = plain(stacked[0 : 256 - 16 * n, :], toep[1024 * n : 1024 * n + 1024, :])
            if n:
                acc[16 * n : 256, :] += term
            else:
                acc[...] = term
        done = acc[...].reshape(32, 8, COLS)
        low = done[:, :, :HALF]
        high = done[:, :, HALF:]
        return jnp.where(first3, low, swap4(high)), jnp.where(first3, swap4(low), high)

    def give(ref, one, two):
        ref[...] = jnp.concatenate([one, two], axis=1).reshape(CTX, 8, HALF).astype(BF)

    wait_all(recv_g, 1, all_rcv)
    even, odd = halves(recv_g)
    rows_g = rows_of(even, odd)
    one, two = convolve(rows_g)
    give(ret_f, one, two)
    scatter(ret_f, back_f, 3)
    gct[...] = jnp.transpose(rows_g).astype(BF)

    wait_all(recv_l, 2, all_rcv)
    even, odd = halves(recv_l)
    one, two = convolve(rows_of(backwards(odd), backwards(even)))
    give(ret_b, backwards(two), backwards(one))
    scatter(ret_b, back_b, 4)

    straight = rows_of(even, odd)
    next_even = jnp.concatenate([even[1:], jnp.zeros((1, 8, HALF), F32)], axis=0)
    crossed = rows_of(odd, next_even)
    zero8 = jnp.zeros((8, COLS), F32)
    for n, value in enumerate(
        (straight, crossed, jnp.concatenate([straight[8:], zero8], axis=0), jnp.concatenate([crossed[8:], zero8], axis=0))
    ):
        gls[n, 0:256, :] = value.astype(BF)
        gls[n, 256:512, :] = jnp.zeros((256, COLS), BF)
    later = cols128 > rows128

    def roll_up(block):
        return pltpu.roll(block, 1, 1, stride=1, stride_axis=0)

    def lag_row(now, last):
        return jnp.sum(jnp.where(later, now, last), axis=0, keepdims=True).reshape(1, 1, HALF)

    def correlate(width):
        def body(m, carry):
            c11, last = carry
            for u in range(4):
                c = plain(gct[:, 0:width], gls[u, pl.ds(pl.multiple_of(16 * m, 16), width), :])
                r0 = roll_up(c11 + c[:HALF, :HALF])
                r1 = roll_up(c[:HALF, HALF:] + c[HALF:, :HALF])
                lag_out[pl.ds(8 * m + 2 * u, 1)] = lag_row(r0, last)
                lag_out[pl.ds(8 * m + 2 * u + 1, 1)] = lag_row(r1, r0)
                c11 = c[HALF:, HALF:]
                last = r1
            return c11, last

        return body

    nothing = jnp.zeros((HALF, HALF), F32)
    c11, last = lax.fori_loop(0, 6, correlate(256), (nothing, nothing))
    kept[0] = c11
    kept[1] = last

    slot_t = iota((COLS, 512), 1)
    chan_t = iota((COLS, 512), 0)
    home_t = (slot_t // 8) * 4 + lax.rem(slot_t, 8)
    take_a = one_hot((home_t == chan_t) & (lax.rem(slot_t, 8) < 4))
    take_b = one_hot((home_t == chan_t + 4) & (lax.rem(slot_t, 8) >= 4))
    same = one_hot(iota((ROWS, ROWS), 0) == iota((ROWS, ROWS), 1))

    def channels(ref):
        got = ref[...].astype(F32).reshape(512, HALF).astype(BF)
        return jnp.concatenate([plain(take_a, got), plain(take_b, got)], axis=1).astype(BF)

    wait_all(back_f, 3, all_rcv)
    long_out = across(flip, channels(back_f))
    y_all = so[0] * long_out
    y_hi = y_all.astype(BF)
    y_lo = (y_all - y_hi.astype(F32)).astype(BF)
    y_t[0] = across(same, y_hi).astype(BF)
    y_t[1] = across(same, y_lo).astype(BF)
    off = pl.multiple_of(other * HALF, HALF)
    mine = pl.multiple_of(dp * HALF, HALF)
    pair_copies = []
    for i in range(TP):
        pair_out[i] = (
            plain(y_t[0, pl.ds(off, HALF), :], cot_all[i]) + plain(y_t[1, pl.ds(off, HALF), :], cot_all[i])
        ).astype(BF)
        c = copy(pair_out.at[i], pair_in.at[i], 8 + i, {"dp": other})
        c.start()
        pair_copies.append(c)
    for i in range(TP):
        part[:, 256 * i : 256 * i + 256] = plain(y_t[0, pl.ds(mine, HALF), :], cot_all[i]) + plain(
            y_t[1, pl.ds(mine, HALF), :], cot_all[i]
        )
    mix_copies = []
    for i in range(TP):
        mix_out[i] = (
            plain(y_hi, w_ref[:, 256 * i : 256 * i + 256]) + plain(y_lo, w_ref[:, 256 * i : 256 * i + 256])
        ).astype(BF)
    for k in range(1, TP):
        c = copy(mix_out.at[peer_tp(k)], mix_in.at[tp], 4 + k, {"tp": peer_tp(k)})
        c.start()
        mix_copies.append(c)

    for i in range(TP):
        pair_copies[i].wait()
        both = part[:, 256 * i : 256 * i + 256] + pair_in[i].astype(F32)
        for r in range(8):
            for h in range(2):
                sum_out[8 * r + 2 * i + h] = both[16 * r : 16 * r + 16, HALF * h : HALF * h + HALF].astype(BF)
    scatter(sum_out, sum_in, 6)

    c11, last = lax.fori_loop(6, 8, correlate(256), (kept[0], kept[1]))
    c11, last = lax.fori_loop(8, 16, correlate(128), (c11, last))
    r0 = roll_up(c11)
    lag_out[128:129] = lag_row(r0, last)
    lag_out[129:130] = lag_row(nothing, r0)

    def send_lags(k, carry):
        peer = peer_ctx(k)
        pltpu.make_async_remote_copy(
            lag_out.at[pl.ds(2 * peer + 2, 2)], lag_in.at[ctx], all_snd.at[5], all_rcv.at[5],
            device_id={"ctx": peer}, device_id_type=MESH,
        ).start()
        return carry

    lax.fori_loop(1, CTX, send_lags, 0)
    lag_in[pl.ds(ctx, 1)] = lag_out[pl.ds(2 * ctx + 2, 2)].reshape(1, 2, 1, HALF)

    wait_all(back_b, 4, all_rcv)
    grad_gated = across(same, channels(back_b))
    edge_out[6:8, :] = jnp.zeros((2, COLS), F32)
    sm0[0, 9:16, :] = jnp.zeros((7, COLS), F32)
    for i in range(3):
        gso = (gy[...] * long_out, grad_gated * so[2], grad_gated * so[1])[i]
        z1 = gso * masks[0]
        z2 = gso * masks[1]
        f0, f1, f2 = (taps_ref[i, s : s + 1, :] for s in range(TAPS))
        edge_out[2 * i : 2 * i + 1, :] = f2 * z2[0:1]
        edge_out[2 * i + 1 : 2 * i + 2, :] = f1 * z1[0:1] + f2 * z2[1:2]
        zbuf[0, 0:ROWS, :] = z1
        zbuf[1, 0:ROWS, :] = z2
        zbuf[:, ROWS : ROWS + 8, :] = jnp.zeros((2, 8, COLS), F32)
        sm0[0, 3 * i : 3 * i + 1, :] = jnp.sum(gso * xe[i, 8 : 8 + ROWS, :], axis=0, keepdims=True)
        sm0[0, 3 * i + 1 : 3 * i + 2, :] = jnp.sum(z1 * xe[i, 7 : 7 + ROWS, :], axis=0, keepdims=True)
        sm0[0, 3 * i + 2 : 3 * i + 3, :] = jnp.sum(z2 * xe[i, 6 : 6 + ROWS, :], axis=0, keepdims=True)
        xe[i, 0:ROWS, :] = f0 * gso + f1 * zbuf[0, 1 : 1 + ROWS, :] + f2 * zbuf[1, 2 : 2 + ROWS, :]
    edge_copy = copy(edge_out, edge_in, 15, {"ctx": peer_ctx(CTX - 1)})
    edge_copy.start()
    small_pair = copy(sm0.at[0], sm0.at[1], 16, {"dp": other})
    small_pair.start()

    wait_all(sum_in, 6, all_rcv)
    total = sum_in[0].astype(F32)
    for n in range(1, CTX):
        total += sum_in[n].astype(F32)
    one_tile[...] = (total * scale).astype(BF)

    def share(k, carry):
        pltpu.make_async_remote_copy(
            one_tile, tiles.at[ctx], all_snd.at[7], grp.at[ctx // 16],
            device_id={"ctx": peer_ctx(k)}, device_id_type=MESH,
        ).start()
        return carry

    lax.fori_loop(1, CTX, share, 0)
    pltpu.make_async_copy(one_tile, tiles.at[ctx], grp.at[ctx // 16]).start()

    small_pair.wait()
    sm1[0] = sm0[0] + sm0[1]
    small_first = []
    for k in range(1, 8):
        c = copy(sm1.at[0], sm1.at[k], 23 + k, dev1(k))
        c.start()
        small_first.append(c)
    edge_copy.wait()
    for i in range(3):
        xe[i, ROWS - 2 : ROWS, :] += edge_in[2 * i : 2 * i + 2, :]
        gin_ref[i] = xe[i, 0:ROWS, :].astype(BF)
    for c in mix_copies:
        c.wait()
    total = mix_out[pl.ds(tp, 1)].astype(F32)
    for k in range(1, TP):
        total += mix_in[pl.ds(peer_tp(k), 1)].astype(F32)
    mixed_ref[...] = total.reshape(ROWS, COLS).astype(BF)
    for c in small_first:
        c.wait()
    small = sm1[0]
    for k in range(1, 8):
        small += sm1[k]
    sm2[0] = small
    small_second = []
    for k in range(1, 8):
        c = copy(sm2.at[0], sm2.at[k], 38 + k, dev2(k))
        c.start()
        small_second.append(c)

    wait_all(lag_in, 5, all_rcv)
    for g in range(16):
        for h in range(2):
            value = lag_in[4 * g, h] + lag_in[4 * g + 1, h] + lag_in[4 * g + 2, h] + lag_in[4 * g + 3, h]
            lag_pair[0, g : g + 1, HALF * h : HALF * h + HALF] = value
    lag_copy = copy(lag_pair.at[0], lag_pair.at[1], 31, {"dp": other})
    lag_copy.start()

    last_copies = []
    for q in range(4):
        group = pl.ds(16 * q, 16)
        pltpu.make_async_copy(tiles.at[group], tiles.at[group], grp.at[q]).wait()
        c = copy(tiles.at[group], tiles_in.at[group], 17 + q, {"dp": other})
        c.start()
        last_copies.append(c)
    for q in range(CTX):
        gproj_ref[pl.ds(pl.multiple_of(mine + 16 * (q // 8), 16), 16), HALF * (q % 8) : HALF * (q % 8) + HALF] = tiles[q]
    lag_copy.wait()
    glong_ref[...] = (lag_pair[0] + lag_pair[1]) * scale
    for c in small_second:
        c.wait()
    small = sm2[0]
    for k in range(1, 8):
        small += sm2[k]
    small = small * scale
    for i in range(3):
        gtaps_ref[i] = small[3 * i : 3 * i + 3, :]
    for n, buf in enumerate((filt_in, send_g, send_l, ret_f, ret_b, lag_in, sum_in, tiles)):
        wait_all(buf, n, all_snd)
    for c in last_copies:
        c.wait()
    for q in range(CTX):
        gproj_ref[pl.ds(pl.multiple_of(off + 16 * (q // 8), 16), 16), HALF * (q % 8) : HALF * (q % 8) + HALF] = tiles_in[q]


def store(mixed, gin, gtaps, glong, gproj, mixed_o, gin_o, gtaps_o, glong_o, gproj_o, wide, sem):
    copies = []
    for n, (src, dst) in enumerate(((gin, gin_o), (mixed, mixed_o), (glong, glong_o), (gtaps, gtaps_o))):
        c = pltpu.make_async_copy(src, dst, sem.at[n])
        c.start()
        copies.append(c)
    for n in range(2):
        rows = pl.ds(HALF * n, HALF)
        wide[rows, :] = gproj[rows, :].astype(F32)
        c = pltpu.make_async_copy(wide.at[rows, :], gproj_o.at[rows, :], sem.at[4 + n])
        c.start()
        copies.append(c)
    for c in copies:
        c.wait()


def per_device(projected, segment_ids, short_filter, long_filter, out_proj, mixed_cotangent):
    scale = 1.0 / math.sqrt(2 * ROWS * CTX)
    V = pltpu.VMEM
    spec = pl.BlockSpec(memory_space=pltpu.VMEM)
    mixed, grad_in, grad_taps, grad_long, grad_proj = pl.pallas_call(
        functools.partial(layer, scale),
        out_shape=(
            jax.ShapeDtypeStruct((ROWS, COLS), BF),
            jax.ShapeDtypeStruct((3, ROWS, COLS), BF),
            jax.ShapeDtypeStruct((3, TAPS, COLS), F32),
            jax.ShapeDtypeStruct((16, COLS), F32),
            jax.ShapeDtypeStruct((256, 1024), BF),
        ),
        in_specs=[pl.BlockSpec(memory_space=pltpu.HBM)] * 6,
        out_specs=[spec] * 5,
        scratch_shapes=[
            V((3, ROWS, COLS), BF), V((1, ROWS), jnp.int32), V((3, TAPS, COLS), F32), V((16, COLS), F32), V((256, 1024), BF),
            pltpu.SemaphoreType.DMA((6,)),
            V((TP, ROWS, COLS), BF), V((8, COLS), F32), V((8, COLS), F32),
            V((16, 1, COLS), F32), V((CTX, 1, COLS), F32),
            V((3, ROWS + 8, COLS), F32), V((3, ROWS, COLS), F32), V((2, ROWS, COLS), F32), V((ROWS, COLS), F32),
            V((CTX, 8, HALF), BF), V((CTX, 8, HALF), BF), V((CTX, 8, HALF), BF), V((CTX, 8, HALF), BF),
            V((64 * 256 + 256, 256), BF), V((256, 1024), BF), V((256, 256), F32),
            V((256, 256), BF), V((4, 512, 256), BF), V((2, HALF, HALF), F32), V((130, 1, HALF), F32), V((CTX, 2, 1, HALF), F32),
            V((CTX, 8, HALF), BF), V((CTX, 8, HALF), BF), V((CTX, 8, HALF), BF), V((CTX, 8, HALF), BF),
            V((2, ROWS + 8, COLS), F32), V((2, COLS, ROWS), BF), V((HALF, 1024), F32),
            V((TP, ROWS, COLS), BF), V((TP, ROWS, COLS), BF),
            V((TP, HALF, COLS), BF), V((TP, HALF, COLS), BF),
            V((CTX, 16, HALF), BF), V((CTX, 16, HALF), BF), V((16, HALF), BF), V((CTX, 16, HALF), BF), V((CTX, 16, HALF), BF),
            V((2, 16, COLS), F32), V((8, 16, COLS), F32), V((8, 16, COLS), F32),
            V((8, COLS), F32), V((8, COLS), F32), V((2, 16, COLS), F32),
            pltpu.SemaphoreType.DMA((46,)), pltpu.SemaphoreType.DMA((46,)),
            pltpu.SemaphoreType.DMA((8,)), pltpu.SemaphoreType.DMA((8,)), pltpu.SemaphoreType.DMA((4,)),
        ],
        compiler_params=pltpu.CompilerParams(vmem_limit_bytes=48 << 20, collective_id=0, has_side_effects=True),
        name="layer",
    )(*(pltpu.with_memory_space_constraint(v, pltpu.HBM) for v in (projected[:, 0], segment_ids, short_filter, long_filter, out_proj, mixed_cotangent[0])))
    mixed, grad_in, grad_taps, grad_long, grad_proj = pl.pallas_call(
        store,
        out_shape=(
            jax.ShapeDtypeStruct((ROWS, COLS), BF),
            jax.ShapeDtypeStruct((3, ROWS, COLS), BF),
            jax.ShapeDtypeStruct((3, TAPS, COLS), F32),
            jax.ShapeDtypeStruct((16, COLS), F32),
            jax.ShapeDtypeStruct((256, 1024), F32),
        ),
        in_specs=[spec] * 5,
        out_specs=[pl.BlockSpec(memory_space=pltpu.HBM)] * 5,
        scratch_shapes=[V((256, 1024), F32), pltpu.SemaphoreType.DMA((6,))],
        compiler_params=pltpu.CompilerParams(vmem_limit_bytes=8 << 20),
        name="store",
    )(mixed, grad_in, grad_taps, grad_long, grad_proj)
    return (mixed[None], grad_in[:, None], grad_taps, grad_long, grad_proj)


def solution(mesh):
    in_specs = (
        P(None, "dp", "ctx", "tp"),
        P("dp", "ctx"),
        P(None, None, "tp"),
        P("tp", "ctx"),
        P("tp", None),
        P("dp", "ctx", "tp"),
    )
    out_specs = (
        P("dp", "ctx", "tp"),
        P(None, "dp", "ctx", "tp"),
        P(None, None, "tp"),
        P("tp", "ctx"),
        P("tp", None),
    )
    return jax.shard_map(
        per_device, mesh=mesh, in_specs=in_specs, out_specs=out_specs, check_vma=False
    )
```

time: 87.6 us -> 73.5 us (0.84)
  local copies, waits for them, and re-layouts: 7.65 us -> 0 us
  Pallas kernels: 77.8 us -> 72.7 us
  other arithmetic: 1.09 us -> 0 us
    unnamed x15 -> x0, local copies, waits for them, and re-layouts: 7.04 us -> none
    pallas_call x1, Pallas kernels: 77.8 us -> 71.5 us  [per_device(): pl.pallas_call(functools.partial(layer, scale), out_shape=(jax.ShapeDtype...]
    pallas_call x0 -> x1, Pallas kernels: none -> 1.2 us  [per_device(): pl.pallas_call(store, out_shape=(jax.ShapeDtypeStruct((ROWS, COLS), BF),...]
    convert_element_type x1 -> x0, other arithmetic: 1.09 us -> none  [per_device(): grad_proj.astype(F32)]
where the time goes in v3:
time: 73.5 us; the launch traced here: 73.3 us
  Pallas kernels  72.7 us (99%)
    pallas_call x1, Pallas kernels, per_device(): pl.pallas_call(functools.partial(layer, scale), out_shape=(jax.ShapeDtype...  71.5 us

profile of v3, /device:TPU:1, one launch (start us, length us, event | category | flops | bytes accessed | tf_op | source)
XLA Modules:
  0.0 73.3 jit_solution(3890039354434967896)
XLA Ops:
  0.6 71.5 %layer.1 = (bf16[256,256]{1,0:T(8,128)(2,1)S(1)}, bf16[3,256,256]{2,1,0:T(8,128)(2,1)S(1)}, f32[3,3,256]{2,1,0:T(4,128)S(1)}, f32[16,256]{1,0:T(8,128)S(1)}, bf16[256,1024]{1,0:T(8,128)(2,1)S(1)}) custom-call(bf16[3,256,256]{2,1,0:T(8,128)(2,1)} %bitcast.6, s32[1,256]{1,0:T(1,128)} %seg_hbm.1, f32[3,3,256]{2,1,0:T(4,128)} %taps_hbm.1, f32[16,256]{1,0:T(8,128)} %filt_hbm.1, ...), custom_call_target="tpu_custom_call" | custom-call | tf_op jit(solution)/shard_map/layer/pallas_call | solution.py:508
  72.1 1.2 %store.1 = (bf16[256,256]{1,0:T(8,128)(2,1)}, bf16[3,256,256]{2,1,0:T(8,128)(2,1)}, f32[3,3,256]{2,1,0:T(4,128)}, f32[16,256]{1,0:T(8,128)}, f32[256,1024]{1,0:T(8,128)}) custom-call(bf16[256,256]{1,0:T(8,128)(2,1)S(1)} %get-tuple-element.15.mixed, bf16[3,256,256]{2,1,0:T(8,128)(2,1)S(1)} %get-tuple-element.16.gin, ...), custom_call_target="tpu_custom_call" | custom-call | tf_op jit(solution)/shard_map/store/pallas_call | solution.py:541

commit v4 on v3

--- a/solution.py
+++ b/solution.py
@@ -39,9 +39,9 @@
     scale,
     x_hbm, seg_hbm, taps_hbm, filt_hbm, w_hbm, cot_hbm,
     mixed_ref, gin_ref, gtaps_ref, glong_ref, gproj_ref,
-    x_ref, seg_ref, taps_ref, filt_ref, w_ref, load_sem,
+    x_ref, seg_ref, taps_ref, filt_ref, w_ref, load_sem, picks, flips,
     cot_all, halo_out, halo_in, filt_out, filt_in, xe, so, masks, gy,
-    send_g, recv_g, send_l, recv_l, toep, stacked, acc, gct, gls, kept, lag_out, lag_in,
+    send_g, recv_g, send_l, recv_l, toep, stacked, acc, gct, gls, lag_out, lag_in,
     ret_f, back_f, ret_b, back_b, zbuf, y_t, part, mix_out, mix_in,
     pair_out, pair_in, sum_out, sum_in, one_tile, tiles, tiles_in,
     sm0, sm1, sm2, edge_out, edge_in, lag_pair,
@@ -78,6 +78,13 @@
     def peer_ctx(k):
         return lax.rem(ctx + k, CTX)
 
+    def reach(k):
+        half = (k + 1) // 2
+        return 4 + half * (2 * lax.rem(k + 1, 2) - 1)
+
+    def peer_far(k):
+        return lax.rem(z + reach(k // 8), 8) * 8 + lax.rem(y + reach(lax.rem(k, 8)), 8)
+
     def copy(src, dst, n, dev):
         return pltpu.make_async_remote_copy(
             src, dst, snd.at[n], rcv.at[n], device_id=dev, device_id_type=MESH
@@ -86,13 +93,13 @@
     barrier = pltpu.get_barrier_semaphore()
 
     def greet(k, carry):
-        pl.semaphore_signal(barrier, 1, device_id={"ctx": peer_ctx(k)}, device_id_type=MESH)
+        pl.semaphore_signal(barrier, 1, device_id={"ctx": peer_far(k)}, device_id_type=MESH)
         return carry
 
     for k in range(1, TP):
         pl.semaphore_signal(barrier, 1, device_id={"tp": peer_tp(k)}, device_id_type=MESH)
     pl.semaphore_signal(barrier, 1, device_id={"dp": other}, device_id_type=MESH)
-    lax.fori_loop(1, CTX, greet, 0)
+    lax.fori_loop(0, CTX - 1, greet, 0)
     loads = []
     for n, (src, dst) in enumerate((
         (filt_hbm, filt_ref), (seg_hbm, seg_ref), (x_hbm, x_ref),
@@ -115,6 +122,15 @@
     seg_col = jnp.transpose(jnp.broadcast_to(seg_row, (HALF, ROWS)))
     halo_out[0:6, :] = jnp.concatenate([x_ref[i, ROWS - 2 : ROWS, :].astype(F32) for i in range(3)], axis=0)
     halo_out[6:8, :] = jnp.concatenate([seg_col[ROWS - 2 : ROWS, :]] * 2, axis=1)
+    slot = iota((512, COLS), 0)
+    chan = iota((512, COLS), 1)
+    home = (slot // 8) * 4 + lax.rem(slot, 8)
+    picks[0] = one_hot((home == chan) & (lax.rem(slot, 8) < 4))
+    picks[1] = one_hot((home == chan + 4) & (lax.rem(slot, 8) >= 4))
+    flips[0] = one_hot(iota((ROWS, ROWS), 0) + iota((ROWS, ROWS), 1) == ROWS - 1)
+    flips[1] = one_hot(iota((ROWS, ROWS), 0) == iota((ROWS, ROWS), 1))
+    for i in range(3):
+        xe[i, 8 : 8 + ROWS, :] = x_ref[i].astype(F32)
     loads[3].wait()
     pl.semaphore_wait(barrier, CTX - 1 + TP - 1 + 1)
 
@@ -127,21 +143,19 @@
         cot_copies.append(c)
 
     def send_filter(k, carry):
-        peer = peer_ctx(k)
+        peer = peer_far(k)
         pltpu.make_async_remote_copy(
             filt_out.at[peer // 4], filt_in.at[ctx], all_snd.at[0], all_rcv.at[0],
             device_id={"ctx": peer}, device_id_type=MESH,
         ).start()
         return carry
 
-    lax.fori_loop(1, CTX, send_filter, 0)
+    lax.fori_loop(0, CTX - 1, send_filter, 0)
     filt_in[pl.ds(ctx, 1)] = filt_out[pl.ds(ctx // 4, 1)]
 
     def wait_all(buf, n, which):
         pltpu.make_async_copy(buf.at[pl.ds(0, CTX - 1)], buf.at[pl.ds(0, CTX - 1)], which.at[n]).wait()
 
-    for i in range(3):
-        xe[i, 8 : 8 + ROWS, :] = x_ref[i].astype(F32)
     halo.wait()
     loads[4].wait()
     loads[5].wait()
@@ -167,27 +181,20 @@
 
     def scatter(src, dst, n):
         def one(k, carry):
-            peer = peer_ctx(k)
+            peer = peer_far(k)
             pltpu.make_async_remote_copy(
                 src.at[peer], dst.at[ctx], all_snd.at[n], all_rcv.at[n],
                 device_id={"ctx": peer}, device_id_type=MESH,
             ).start()
             return carry
 
-        lax.fori_loop(1, CTX, one, 0)
+        lax.fori_loop(0, CTX - 1, one, 0)
         dst[pl.ds(ctx, 1)] = src[pl.ds(ctx, 1)]
 
-    slot = iota((512, COLS), 0)
-    chan = iota((512, COLS), 1)
-    home = (slot // 8) * 4 + lax.rem(slot, 8)
-    pick_a = one_hot((home == chan) & (lax.rem(slot, 8) < 4))
-    pick_b = one_hot((home == chan + 4) & (lax.rem(slot, 8) >= 4))
-    flip = one_hot(iota((ROWS, ROWS), 0) + iota((ROWS, ROWS), 1) == ROWS - 1)
-
     def tiles_of(value):
-        return (across(pick_a, value[:HALF]) + across(pick_b, value[HALF:])).reshape(CTX, 8, HALF).astype(BF)
-
-    send_g[...] = tiles_of(plain(flip, (so[1] * so[2]).astype(BF)).astype(BF))
+        return (across(picks[0], value[:HALF]) + across(picks[1], value[HALF:])).reshape(CTX, 8, HALF).astype(BF)
+
+    send_g[...] = tiles_of(plain(flips[0], (so[1] * so[2]).astype(BF)).astype(BF))
     scatter(send_g, recv_g, 1)
     featurize(0)
 
@@ -278,56 +285,19 @@
     give(ret_b, backwards(two), backwards(one))
     scatter(ret_b, back_b, 4)
 
-    straight = rows_of(even, odd)
-    next_even = jnp.concatenate([even[1:], jnp.zeros((1, 8, HALF), F32)], axis=0)
-    crossed = rows_of(odd, next_even)
-    zero8 = jnp.zeros((8, COLS), F32)
-    for n, value in enumerate(
-        (straight, crossed, jnp.concatenate([straight[8:], zero8], axis=0), jnp.concatenate([crossed[8:], zero8], axis=0))
-    ):
-        gls[n, 0:256, :] = value.astype(BF)
-        gls[n, 256:512, :] = jnp.zeros((256, COLS), BF)
-    later = cols128 > rows128
-
-    def roll_up(block):
-        return pltpu.roll(block, 1, 1, stride=1, stride_axis=0)
-
-    def lag_row(now, last):
-        return jnp.sum(jnp.where(later, now, last), axis=0, keepdims=True).reshape(1, 1, HALF)
-
-    def correlate(width):
-        def body(m, carry):
-            c11, last = carry
-            for u in range(4):
-                c = plain(gct[:, 0:width], gls[u, pl.ds(pl.multiple_of(16 * m, 16), width), :])
-                r0 = roll_up(c11 + c[:HALF, :HALF])
-                r1 = roll_up(c[:HALF, HALF:] + c[HALF:, :HALF])
-                lag_out[pl.ds(8 * m + 2 * u, 1)] = lag_row(r0, last)
-                lag_out[pl.ds(8 * m + 2 * u + 1, 1)] = lag_row(r1, r0)
-                c11 = c[HALF:, HALF:]
-                last = r1
-            return c11, last
-
-        return body
-
-    nothing = jnp.zeros((HALF, HALF), F32)
-    c11, last = lax.fori_loop(0, 6, correlate(256), (nothing, nothing))
-    kept[0] = c11
-    kept[1] = last
-
     slot_t = iota((COLS, 512), 1)
     chan_t = iota((COLS, 512), 0)
     home_t = (slot_t // 8) * 4 + lax.rem(slot_t, 8)
     take_a = one_hot((home_t == chan_t) & (lax.rem(slot_t, 8) < 4))
     take_b = one_hot((home_t == chan_t + 4) & (lax.rem(slot_t, 8) >= 4))
-    same = one_hot(iota((ROWS, ROWS), 0) == iota((ROWS, ROWS), 1))
+    same = flips[1]
 
     def channels(ref):
         got = ref[...].astype(F32).reshape(512, HALF).astype(BF)
         return jnp.concatenate([plain(take_a, got), plain(take_b, got)], axis=1).astype(BF)
 
     wait_all(back_f, 3, all_rcv)
-    long_out = across(flip, channels(back_f))
+    long_out = across(flips[0], channels(back_f))
     y_all = so[0] * long_out
     y_hi = y_all.astype(BF)
     y_lo = (y_all - y_hi.astype(F32)).astype(BF)
@@ -364,23 +334,6 @@
             for h in range(2):
                 sum_out[8 * r + 2 * i + h] = both[16 * r : 16 * r + 16, HALF * h : HALF * h + HALF].astype(BF)
     scatter(sum_out, sum_in, 6)
-
-    c11, last = lax.fori_loop(6, 8, correlate(256), (kept[0], kept[1]))
-    c11, last = lax.fori_loop(8, 16, correlate(128), (c11, last))
-    r0 = roll_up(c11)
-    lag_out[128:129] = lag_row(r0, last)
-    lag_out[129:130] = lag_row(nothing, r0)
-
-    def send_lags(k, carry):
-        peer = peer_ctx(k)
-        pltpu.make_async_remote_copy(
-            lag_out.at[pl.ds(2 * peer + 2, 2)], lag_in.at[ctx], all_snd.at[5], all_rcv.at[5],
-            device_id={"ctx": peer}, device_id_type=MESH,
-        ).start()
-        return carry
-
-    lax.fori_loop(1, CTX, send_lags, 0)
-    lag_in[pl.ds(ctx, 1)] = lag_out[pl.ds(2 * ctx + 2, 2)].reshape(1, 2, 1, HALF)
 
     wait_all(back_b, 4, all_rcv)
     grad_gated = across(same, channels(back_b))
@@ -405,6 +358,57 @@
     small_pair = copy(sm0.at[0], sm0.at[1], 16, {"dp": other})
     small_pair.start()
 
+    straight = rows_of(even, odd)
+    next_even = jnp.concatenate([even[1:], jnp.zeros((1, 8, HALF), F32)], axis=0)
+    crossed = rows_of(odd, next_even)
+    zero8 = jnp.zeros((8, COLS), F32)
+    for n, value in enumerate(
+        (straight, crossed, jnp.concatenate([straight[8:], zero8], axis=0), jnp.concatenate([crossed[8:], zero8], axis=0))
+    ):
+        gls[n, 0:256, :] = value.astype(BF)
+        gls[n, 256:512, :] = jnp.zeros((256, COLS), BF)
+    later = cols128 > rows128
+
+    def roll_up(block):
+        return pltpu.roll(block, 1, 1, stride=1, stride_axis=0)
+
+    def lag_row(now, last):
+        return jnp.sum(jnp.where(later, now, last), axis=0, keepdims=True).reshape(1, 1, HALF)
+
+    def correlate(width):
+        def body(m, carry):
+            c11, last = carry
+            for u in range(4):
+                c = plain(gct[:, 0:width], gls[u, pl.ds(pl.multiple_of(16 * m, 16), width), :])
+                r0 = roll_up(c11 + c[:HALF, :HALF])
+                r1 = roll_up(c[:HALF, HALF:] + c[HALF:, :HALF])
+                lag_out[pl.ds(8 * m + 2 * u, 1)] = lag_row(r0, last)
+                lag_out[pl.ds(8 * m + 2 * u + 1, 1)] = lag_row(r1, r0)
+                c11 = c[HALF:, HALF:]
+                last = r1
+            return c11, last
+
+        return body
+
+    nothing = jnp.zeros((HALF, HALF), F32)
+
+    c11, last = lax.fori_loop(0, 8, correlate(256), (nothing, nothing))
+    c11, last = lax.fori_loop(8, 16, correlate(128), (c11, last))
+    r0 = roll_up(c11)
+    lag_out[128:129] = lag_row(r0, last)
+    lag_out[129:130] = lag_row(nothing, r0)
+
+    def send_lags(k, carry):
+        peer = peer_far(k)
+        pltpu.make_async_remote_copy(
+            lag_out.at[pl.ds(2 * peer + 2, 2)], lag_in.at[ctx], all_snd.at[5], all_rcv.at[5],
+            device_id={"ctx": peer}, device_id_type=MESH,
+        ).start()
+        return carry
+
+    lax.fori_loop(0, CTX - 1, send_lags, 0)
+    lag_in[pl.ds(ctx, 1)] = lag_out[pl.ds(2 * ctx + 2, 2)].reshape(1, 2, 1, HALF)
+
     wait_all(sum_in, 6, all_rcv)
     total = sum_in[0].astype(F32)
     for n in range(1, CTX):
@@ -414,11 +418,11 @@
     def share(k, carry):
         pltpu.make_async_remote_copy(
             one_tile, tiles.at[ctx], all_snd.at[7], grp.at[ctx // 16],
-            device_id={"ctx": peer_ctx(k)}, device_id_type=MESH,
+            device_id={"ctx": peer_far(k)}, device_id_type=MESH,
         ).start()
         return carry
 
-    lax.fori_loop(1, CTX, share, 0)
+    lax.fori_loop(0, CTX - 1, share, 0)
     pltpu.make_async_copy(one_tile, tiles.at[ctx], grp.at[ctx // 16]).start()
 
     small_pair.wait()
@@ -518,13 +522,13 @@
         out_specs=[spec] * 5,
         scratch_shapes=[
             V((3, ROWS, COLS), BF), V((1, ROWS), jnp.int32), V((3, TAPS, COLS), F32), V((16, COLS), F32), V((256, 1024), BF),
-            pltpu.SemaphoreType.DMA((6,)),
+            pltpu.SemaphoreType.DMA((6,)), V((2, 512, COLS), BF), V((2, ROWS, ROWS), BF),
             V((TP, ROWS, COLS), BF), V((8, COLS), F32), V((8, COLS), F32),
             V((16, 1, COLS), F32), V((CTX, 1, COLS), F32),
             V((3, ROWS + 8, COLS), F32), V((3, ROWS, COLS), F32), V((2, ROWS, COLS), F32), V((ROWS, COLS), F32),
             V((CTX, 8, HALF), BF), V((CTX, 8, HALF), BF), V((CTX, 8, HALF), BF), V((CTX, 8, HALF), BF),
             V((64 * 256 + 256, 256), BF), V((256, 1024), BF), V((256, 256), F32),
-            V((256, 256), BF), V((4, 512, 256), BF), V((2, HALF, HALF), F32), V((130, 1, HALF), F32), V((CTX, 2, 1, HALF), F32),
+            V((256, 256), BF), V((4, 512, 256), BF), V((130, 1, HALF), F32), V((CTX, 2, 1, HALF), F32),
             V((CTX, 8, HALF), BF), V((CTX, 8, HALF), BF), V((CTX, 8, HALF), BF), V((CTX, 8, HALF), BF),
             V((2, ROWS + 8, COLS), F32), V((2, COLS, ROWS), BF), V((HALF, 1024), F32),
             V((TP, ROWS, COLS), BF), V((TP, ROWS, COLS), BF),

time: 73.5 us -> 73.9 us (level)
  no operation moved by 1% of the time
where the time goes in v4:
time: 73.9 us; the launch traced here: 73.8 us
  Pallas kernels  73.1 us (99%)
    pallas_call x1, Pallas kernels, per_device(): pl.pallas_call(functools.partial(layer, scale), out_shape=(jax.ShapeDtype...  71.9 us

profile of v4, /device:TPU:1, one launch (start us, length us, event | category | flops | bytes accessed | tf_op | source)
XLA Modules:
  0.0 73.8 jit_solution(14815085300387357573)
XLA Ops:
  0.6 71.9 %layer.1 = (bf16[256,256]{1,0:T(8,128)(2,1)S(1)}, bf16[3,256,256]{2,1,0:T(8,128)(2,1)S(1)}, f32[3,3,256]{2,1,0:T(4,128)S(1)}, f32[16,256]{1,0:T(8,128)S(1)}, bf16[256,1024]{1,0:T(8,128)(2,1)S(1)}) custom-call(bf16[3,256,256]{2,1,0:T(8,128)(2,1)} %bitcast.6, s32[1,256]{1,0:T(1,128)} %seg_hbm.1, f32[3,3,256]{2,1,0:T(4,128)} %taps_hbm.1, f32[16,256]{1,0:T(8,128)} %filt_hbm.1, ...), custom_call_target="tpu_custom_call" | custom-call | tf_op jit(solution)/shard_map/layer/pallas_call | solution.py:512
  72.6 1.2 %store.1 = (bf16[256,256]{1,0:T(8,128)(2,1)}, bf16[3,256,256]{2,1,0:T(8,128)(2,1)}, f32[3,3,256]{2,1,0:T(4,128)}, f32[16,256]{1,0:T(8,128)}, f32[256,1024]{1,0:T(8,128)}) custom-call(bf16[256,256]{1,0:T(8,128)(2,1)S(1)} %get-tuple-element.15.mixed, bf16[3,256,256]{2,1,0:T(8,128)(2,1)S(1)} %get-tuple-element.16.gin, ...), custom_call_target="tpu_custom_call" | custom-call | tf_op jit(solution)/shard_map/store/pallas_call | solution.py:545

commit v5 on v4

--- a/solution.py
+++ b/solution.py
@@ -41,7 +41,7 @@
     mixed_ref, gin_ref, gtaps_ref, glong_ref, gproj_ref,
     x_ref, seg_ref, taps_ref, filt_ref, w_ref, load_sem, picks, flips,
     cot_all, halo_out, halo_in, filt_out, filt_in, xe, so, masks, gy,
-    send_g, recv_g, send_l, recv_l, toep, stacked, acc, gct, gls, lag_out, lag_in,
+    send_g, recv_g, send_l, recv_l, toep, stacked, acc, gct, gls, kept, lag_out, lag_in,
     ret_f, back_f, ret_b, back_b, zbuf, y_t, part, mix_out, mix_in,
     pair_out, pair_in, sum_out, sum_in, one_tile, tiles, tiles_in,
     sm0, sm1, sm2, edge_out, edge_in, lag_pair,
@@ -78,12 +78,8 @@
     def peer_ctx(k):
         return lax.rem(ctx + k, CTX)
 
-    def reach(k):
-        half = (k + 1) // 2
-        return 4 + half * (2 * lax.rem(k + 1, 2) - 1)
-
-    def peer_far(k):
-        return lax.rem(z + reach(k // 8), 8) * 8 + lax.rem(y + reach(lax.rem(k, 8)), 8)
+    def peer_nth(k):
+        return lax.rem(ctx + k + 1, CTX)
 
     def copy(src, dst, n, dev):
         return pltpu.make_async_remote_copy(
@@ -93,7 +89,7 @@
     barrier = pltpu.get_barrier_semaphore()
 
     def greet(k, carry):
-        pl.semaphore_signal(barrier, 1, device_id={"ctx": peer_far(k)}, device_id_type=MESH)
+        pl.semaphore_signal(barrier, 1, device_id={"ctx": peer_nth(k)}, device_id_type=MESH)
         return carry
 
     for k in range(1, TP):
@@ -143,7 +139,7 @@
         cot_copies.append(c)
 
     def send_filter(k, carry):
-        peer = peer_far(k)
+        peer = peer_nth(k)
         pltpu.make_async_remote_copy(
             filt_out.at[peer // 4], filt_in.at[ctx], all_snd.at[0], all_rcv.at[0],
             device_id={"ctx": peer}, device_id_type=MESH,
@@ -181,7 +177,7 @@
 
     def scatter(src, dst, n):
         def one(k, carry):
-            peer = peer_far(k)
+            peer = peer_nth(k)
             pltpu.make_async_remote_copy(
                 src.at[peer], dst.at[ctx], all_snd.at[n], all_rcv.at[n],
                 device_id={"ctx": peer}, device_id_type=MESH,
@@ -393,13 +389,39 @@
     nothing = jnp.zeros((HALF, HALF), F32)
 
     c11, last = lax.fori_loop(0, 8, correlate(256), (nothing, nothing))
-    c11, last = lax.fori_loop(8, 16, correlate(128), (c11, last))
+    kept[0] = c11
+    kept[1] = last
+
+    wait_all(sum_in, 6, all_rcv)
+    total = sum_in[0].astype(F32)
+    for n in range(1, CTX):
+        total += sum_in[n].astype(F32)
+    one_tile[...] = (total * scale).astype(BF)
+
+    def share(k, carry):
+        pltpu.make_async_remote_copy(
+            one_tile, tiles.at[ctx], all_snd.at[7], grp.at[ctx // 16],
+            device_id={"ctx": peer_nth(k)}, device_id_type=MESH,
+        ).start()
+        return carry
+
+    lax.fori_loop(0, CTX - 1, share, 0)
+    pltpu.make_async_copy(one_tile, tiles.at[ctx], grp.at[ctx // 16]).start()
+
+    small_pair.wait()
+    sm1[0] = sm0[0] + sm0[1]
+    small_first = []
+    for k in range(1, 8):
+        c = copy(sm1.at[0], sm1.at[k], 23 + k, dev1(k))
+        c.start()
+        small_first.append(c)
+    c11, last = lax.fori_loop(8, 16, correlate(128), (kept[0], kept[1]))
     r0 = roll_up(c11)
     lag_out[128:129] = lag_row(r0, last)
     lag_out[129:130] = lag_row(nothing, r0)
 
     def send_lags(k, carry):
-        peer = peer_far(k)
+        peer = peer_nth(k)
         pltpu.make_async_remote_copy(
             lag_out.at[pl.ds(2 * peer + 2, 2)], lag_in.at[ctx], all_snd.at[5], all_rcv.at[5],
             device_id={"ctx": peer}, device_id_type=MESH,
@@ -408,30 +430,6 @@
 
     lax.fori_loop(0, CTX - 1, send_lags, 0)
     lag_in[pl.ds(ctx, 1)] = lag_out[pl.ds(2 * ctx + 2, 2)].reshape(1, 2, 1, HALF)
-
-    wait_all(sum_in, 6, all_rcv)
-    total = sum_in[0].astype(F32)
-    for n in range(1, CTX):
-        total += sum_in[n].astype(F32)
-    one_tile[...] = (total * scale).astype(BF)
-
-    def share(k, carry):
-        pltpu.make_async_remote_copy(
-            one_tile, tiles.at[ctx], all_snd.at[7], grp.at[ctx // 16],
-            device_id={"ctx": peer_far(k)}, device_id_type=MESH,
-        ).start()
-        return carry
-
-    lax.fori_loop(0, CTX - 1, share, 0)
-    pltpu.make_async_copy(one_tile, tiles.at[ctx], grp.at[ctx // 16]).start()
-
-    small_pair.wait()
-    sm1[0] = sm0[0] + sm0[1]
-    small_first = []
-    for k in range(1, 8):
-        c = copy(sm1.at[0], sm1.at[k], 23 + k, dev1(k))
-        c.start()
-        small_first.append(c)
     edge_copy.wait()
     for i in range(3):
         xe[i, ROWS - 2 : ROWS, :] += edge_in[2 * i : 2 * i + 2, :]
@@ -528,7 +526,7 @@
             V((3, ROWS + 8, COLS), F32), V((3, ROWS, COLS), F32), V((2, ROWS, COLS), F32), V((ROWS, COLS), F32),
             V((CTX, 8, HALF), BF), V((CTX, 8, HALF), BF), V((CTX, 8, HALF), BF), V((CTX, 8, HALF), BF),
             V((64 * 256 + 256, 256), BF), V((256, 1024), BF), V((256, 256), F32),
-            V((256, 256), BF), V((4, 512, 256), BF), V((130, 1, HALF), F32), V((CTX, 2, 1, HALF), F32),
+            V((256, 256), BF), V((4, 512, 256), BF), V((2, HALF, HALF), F32), V((130, 1, HALF), F32), V((CTX, 2, 1, HALF), F32),
             V((CTX, 8, HALF), BF), V((CTX, 8, HALF), BF), V((CTX, 8, HALF), BF), V((CTX, 8, HALF), BF),
             V((2, ROWS + 8, COLS), F32), V((2, COLS, ROWS), BF), V((HALF, 1024), F32),
             V((TP, ROWS, COLS), BF), V((TP, ROWS, COLS), BF),

time: 73.9 us -> 71.9 us (0.973)
  Pallas kernels: 73.1 us -> 71 us
    pallas_call x1, Pallas kernels: 71.9 us -> 69.8 us  [per_device(): pl.pallas_call(functools.partial(layer, scale), out_shape=(jax.ShapeDtype...]
where the time goes in v5:
time: 71.9 us; the launch traced here: 71.7 us
  Pallas kernels  71 us (99%)
    pallas_call x1, Pallas kernels, per_device(): pl.pallas_call(functools.partial(layer, scale), out_shape=(jax.ShapeDtype...  69.8 us

profile of v5, /device:TPU:1, one launch (start us, length us, event | category | flops | bytes accessed | tf_op | source)
XLA Modules:
  0.0 71.7 jit_solution(15027656300593350663)
XLA Ops:
  0.6 69.8 %layer.1 = (bf16[256,256]{1,0:T(8,128)(2,1)S(1)}, bf16[3,256,256]{2,1,0:T(8,128)(2,1)S(1)}, f32[3,3,256]{2,1,0:T(4,128)S(1)}, f32[16,256]{1,0:T(8,128)S(1)}, bf16[256,1024]{1,0:T(8,128)(2,1)S(1)}) custom-call(bf16[3,256,256]{2,1,0:T(8,128)(2,1)} %bitcast.6, s32[1,256]{1,0:T(1,128)} %seg_hbm.1, f32[3,3,256]{2,1,0:T(4,128)} %taps_hbm.1, f32[16,256]{1,0:T(8,128)} %filt_hbm.1, ...), custom_call_target="tpu_custom_call" | custom-call | tf_op jit(solution)/shard_map/layer/pallas_call | solution.py:510
  70.5 1.2 %store.1 = (bf16[256,256]{1,0:T(8,128)(2,1)}, bf16[3,256,256]{2,1,0:T(8,128)(2,1)}, f32[3,3,256]{2,1,0:T(4,128)}, f32[16,256]{1,0:T(8,128)}, f32[256,1024]{1,0:T(8,128)}) custom-call(bf16[256,256]{1,0:T(8,128)(2,1)S(1)} %get-tuple-element.15.mixed, bf16[3,256,256]{2,1,0:T(8,128)(2,1)S(1)} %get-tuple-element.16.gin, ...), custom_call_target="tpu_custom_call" | custom-call | tf_op jit(solution)/shard_map/store/pallas_call | solution.py:543

commit v6 on v4

--- a/solution.py
+++ b/solution.py
@@ -78,12 +78,8 @@
     def peer_ctx(k):
         return lax.rem(ctx + k, CTX)
 
-    def reach(k):
-        half = (k + 1) // 2
-        return 4 + half * (2 * lax.rem(k + 1, 2) - 1)
-
-    def peer_far(k):
-        return lax.rem(z + reach(k // 8), 8) * 8 + lax.rem(y + reach(lax.rem(k, 8)), 8)
+    def peer_nth(k):
+        return lax.rem(ctx + k + 1, CTX)
 
     def copy(src, dst, n, dev):
         return pltpu.make_async_remote_copy(
@@ -93,7 +89,7 @@
     barrier = pltpu.get_barrier_semaphore()
 
     def greet(k, carry):
-        pl.semaphore_signal(barrier, 1, device_id={"ctx": peer_far(k)}, device_id_type=MESH)
+        pl.semaphore_signal(barrier, 1, device_id={"ctx": peer_nth(k)}, device_id_type=MESH)
         return carry
 
     for k in range(1, TP):
@@ -143,7 +139,7 @@
         cot_copies.append(c)
 
     def send_filter(k, carry):
-        peer = peer_far(k)
+        peer = peer_nth(k)
         pltpu.make_async_remote_copy(
             filt_out.at[peer // 4], filt_in.at[ctx], all_snd.at[0], all_rcv.at[0],
             device_id={"ctx": peer}, device_id_type=MESH,
@@ -181,7 +177,7 @@
 
     def scatter(src, dst, n):
         def one(k, carry):
-            peer = peer_far(k)
+            peer = peer_nth(k)
             pltpu.make_async_remote_copy(
                 src.at[peer], dst.at[ctx], all_snd.at[n], all_rcv.at[n],
                 device_id={"ctx": peer}, device_id_type=MESH,
@@ -393,13 +389,20 @@
     nothing = jnp.zeros((HALF, HALF), F32)
 
     c11, last = lax.fori_loop(0, 8, correlate(256), (nothing, nothing))
+    small_pair.wait()
+    sm1[0] = sm0[0] + sm0[1]
+    small_first = []
+    for k in range(1, 8):
+        c = copy(sm1.at[0], sm1.at[k], 23 + k, dev1(k))
+        c.start()
+        small_first.append(c)
     c11, last = lax.fori_loop(8, 16, correlate(128), (c11, last))
     r0 = roll_up(c11)
     lag_out[128:129] = lag_row(r0, last)
     lag_out[129:130] = lag_row(nothing, r0)
 
     def send_lags(k, carry):
-        peer = peer_far(k)
+        peer = peer_nth(k)
         pltpu.make_async_remote_copy(
             lag_out.at[pl.ds(2 * peer + 2, 2)], lag_in.at[ctx], all_snd.at[5], all_rcv.at[5],
             device_id={"ctx": peer}, device_id_type=MESH,
@@ -418,20 +421,24 @@
     def share(k, carry):
         pltpu.make_async_remote_copy(
             one_tile, tiles.at[ctx], all_snd.at[7], grp.at[ctx // 16],
-            device_id={"ctx": peer_far(k)}, device_id_type=MESH,
+            device_id={"ctx": peer_nth(k)}, device_id_type=MESH,
         ).start()
         return carry
 
     lax.fori_loop(0, CTX - 1, share, 0)
     pltpu.make_async_copy(one_tile, tiles.at[ctx], grp.at[ctx // 16]).start()
 
-    small_pair.wait()
-    sm1[0] = sm0[0] + sm0[1]
-    small_first = []
+    for c in small_first:
+        c.wait()
+    small = sm1[0]
     for k in range(1, 8):
-        c = copy(sm1.at[0], sm1.at[k], 23 + k, dev1(k))
-        c.start()
-        small_first.append(c)
+        small += sm1[k]
+    sm2[0] = small
+    small_second = []
+    for k in range(1, 8):
+        c = copy(sm2.at[0], sm2.at[k], 38 + k, dev2(k))
+        c.start()
+        small_second.append(c)
     edge_copy.wait()
     for i in range(3):
         xe[i, ROWS - 2 : ROWS, :] += edge_in[2 * i : 2 * i + 2, :]
@@ -442,18 +449,6 @@
     for k in range(1, TP):
         total += mix_in[pl.ds(peer_tp(k), 1)].astype(F32)
     mixed_ref[...] = total.reshape(ROWS, COLS).astype(BF)
-    for c in small_first:
-        c.wait()
-    small = sm1[0]
-    for k in range(1, 8):
-        small += sm1[k]
-    sm2[0] = small
-    small_second = []
-    for k in range(1, 8):
-        c = copy(sm2.at[0], sm2.at[k], 38 + k, dev2(k))
-        c.start()
-        small_second.append(c)
-
     wait_all(lag_in, 5, all_rcv)
     for g in range(16):
         for h in range(2):

time: 73.9 us -> 70.6 us (0.955)
  Pallas kernels: 73.1 us -> 69.8 us
    pallas_call x1, Pallas kernels: 71.9 us -> 68.6 us  [per_device(): pl.pallas_call(functools.partial(layer, scale), out_shape=(jax.ShapeDtype...]
where the time goes in v6:
time: 70.6 us; the launch traced here: 70.4 us
  Pallas kernels  69.8 us (99%)
    pallas_call x1, Pallas kernels, per_device(): pl.pallas_call(functools.partial(layer, scale), out_shape=(jax.ShapeDtype...  68.6 us

profile of v6, /device:TPU:1, one launch (start us, length us, event | category | flops | bytes accessed | tf_op | source)
XLA Modules:
  0.0 70.4 jit_solution(17207446738395644694)
XLA Ops:
  0.6 68.6 %layer.1 = (bf16[256,256]{1,0:T(8,128)(2,1)S(1)}, bf16[3,256,256]{2,1,0:T(8,128)(2,1)S(1)}, f32[3,3,256]{2,1,0:T(4,128)S(1)}, f32[16,256]{1,0:T(8,128)S(1)}, bf16[256,1024]{1,0:T(8,128)(2,1)S(1)}) custom-call(bf16[3,256,256]{2,1,0:T(8,128)(2,1)} %bitcast.6, s32[1,256]{1,0:T(1,128)} %seg_hbm.1, f32[3,3,256]{2,1,0:T(4,128)} %taps_hbm.1, f32[16,256]{1,0:T(8,128)} %filt_hbm.1, ...), custom_call_target="tpu_custom_call" | custom-call | tf_op jit(solution)/shard_map/layer/pallas_call | solution.py:507
  69.2 1.2 %store.1 = (bf16[256,256]{1,0:T(8,128)(2,1)}, bf16[3,256,256]{2,1,0:T(8,128)(2,1)}, f32[3,3,256]{2,1,0:T(4,128)}, f32[16,256]{1,0:T(8,128)}, f32[256,1024]{1,0:T(8,128)}) custom-call(bf16[256,256]{1,0:T(8,128)(2,1)S(1)} %get-tuple-element.15.mixed, bf16[3,256,256]{2,1,0:T(8,128)(2,1)S(1)} %get-tuple-element.16.gin, ...), custom_call_target="tpu_custom_call" | custom-call | tf_op jit(solution)/shard_map/store/pallas_call | solution.py:540
